TPU v7x, 32 devices: a whole 2x2x4 slice. The times are simulated.
32 devices in a mesh: groups: 2 (over y), queue: 8 (over z, x), tp: 2 (over core).
Axes of the slice: x: 2, y: 2, z: 4, core: 2. Of those that a mesh axis runs over, the one named last changes fastest.
Arguments:
- hidden: bfloat16 [3328, 5120], P(('groups', 'queue'), 'tp'), parts along dimension 0, may hold values from -8 to 8
- q_weight: bfloat16 [1, 40, 128, 128], P(None, 'tp'), may hold values from -1 to 2.5
- k_weight: bfloat16 [1, 40, 128, 128], P(None, 'tp'), may hold values from -1 to 2.5
- v_weight: bfloat16 [1, 40, 128, 128], P(None, 'tp'), may hold values from -0.5 to 0.5
- mod_base: float32 [1, 3, 5120], P(None, None, 'tp'), may hold values from -3 to 3
- mod_amp: float32 [1, 3, 5120], P(None, None, 'tp'), may hold values from -3 to 3
- levels: int32 [16], P(('groups', 'queue')), parts along dimension 0, may hold values from 0 to 63
- steps_table: int32 [65], replicated, may hold values from 0 to 1000
- group_pos: int32 [16], P('groups'), parts along dimension 0, may hold values from 0 to 31
Outputs:
- new_queue: bfloat16 [3328, 5120], P(('groups', 'queue'), 'tp'), parts along dimension 0
- velocity: bfloat16 [3328, 5120], P(('groups', 'queue'), 'tp'), parts along dimension 0
There are 2 independent parts, one for each index of `groups`. A program takes and returns all parts, laid end to end along the dimension named above; an argument that names none is the same for every part. Nothing has to cross between parts.
All inputs are finite; a program needn't handle non-finite values.
Results may differ from a plain program's by a relative error of at most 0.0054.
Values may be sent and summed in bfloat16 or wider, within the bound.
No kernel may reach another device: no remote copies, remote signals or barrier semaphores. Data moves between devices by JAX's collectives and lax.ppermute only.
A program may use at most 64 MiB of HBM per device.

v0:
```python
import functools
import math

import jax
import jax.numpy as jnp
from jax import lax
from jax.experimental import pallas as pl
from jax.experimental.pallas import tpu as pltpu
from jax.sharding import PartitionSpec as P

WIDE = 52
HW_DEV = 104
PERIOD = 256
CHUNKS = 2
STEP_HEADS = 2
SUM_HEADS = 4
LIMIT = 24 << 20
F32 = jnp.float32
BF16 = jnp.bfloat16
VMEM = pl.BlockSpec(memory_space=pltpu.VMEM)


def send(array, pairs, length, wrap=False):
    if wrap:
        pairs = [(a, b % length) for a, b in pairs]
    pairs = [(a, b) for a, b in pairs if 0 <= b < length]
    return lax.ppermute(array, "queue", pairs)


def other_core(array):
    if lax.axis_size("tp") == 2:
        return lax.ppermute(array, "tp", [(0, 1), (1, 0)])
    return lax.psum(array, "tp") - array


def divisor(count, most):
    return max(k for k in range(1, most + 1) if count % k == 0)


def time_embed(moment, channel):
    within = channel % 256
    freq = jnp.exp(-jnp.log(10000.0) * (within % 128).astype(F32) / 128.0)
    angle = moment * freq
    return jnp.where(within < 128, jnp.cos(angle), jnp.sin(angle))


def pair_plan(shape, size):
    half = size // 2
    side = size // 6
    lead = (size - 4 * side) // 2
    pair = lax.broadcasted_iota(jnp.int32, shape, len(shape) - 1) % half
    part = jnp.where(pair < lead, 0, jnp.where(pair < lead + side, 1, 2))
    within = pair - jnp.where(part == 0, 0, jnp.where(part == 1, lead, lead + side))
    pairs = jnp.where(part == 0, lead, side).astype(F32)
    return part, jnp.exp(-math.log(10000.0) * (within.astype(F32) / pairs))


def pairs_apart(size):
    row = jnp.arange(size)[:, None]
    col = jnp.arange(size)[None, :]
    half = size // 2
    return (row == 2 * (col % half) + col // half).astype(BF16)


def normed_mix(x, mean, rstd, shift, scale):
    return ((x - mean) * rstd * (1.0 + scale) + shift).astype(BF16)


def to_rows(columns, size):
    count = columns[0].shape[0]
    lane = lax.broadcasted_iota(jnp.int32, (count, size), 1)
    wide = jnp.zeros((count, size), F32)
    for j, column in enumerate(columns):
        wide = jnp.where(lane == j, jnp.broadcast_to(column, (count, size)), wide)
    return jnp.transpose(wide)[:8]


def split_kernel(size, cuts, x_ref, *outs):
    out_ref = outs[-1]
    count, _ = x_ref.shape
    total = jnp.zeros((count, size), F32)
    second = jnp.zeros((count, size), F32)
    for piece, lo, hi in zip(outs, cuts[:-1], cuts[1:]):
        for h in range(lo, hi):
            raw = x_ref[:, h * size : (h + 1) * size]
            piece[:, (h - lo) * size : (h - lo + 1) * size] = raw
            x = raw.astype(F32)
            total += x
            second += x * x
    out_ref[...] = to_rows(
        [jnp.sum(total, axis=1, keepdims=True), jnp.sum(second, axis=1, keepdims=True)], size
    )


def split(x, cuts, size):
    count, width = x.shape
    return pl.pallas_call(
        functools.partial(split_kernel, size, cuts),
        name="token_split",
        in_specs=[VMEM],
        out_specs=[VMEM] * len(cuts),
        out_shape=[jax.ShapeDtypeStruct((count, (hi - lo) * size), BF16) for lo, hi in zip(cuts[:-1], cuts[1:])]
        + [jax.ShapeDtypeStruct((8, count), F32)],
        compiler_params=pltpu.CompilerParams(vmem_limit_bytes=LIMIT),
        cost_estimate=pl.CostEstimate(flops=4 * count * width, bytes_accessed=4 * count * width, transcendentals=0),
    )(x)


def squares_kernel(
    heads, size, width, level_ref, steps_ref,
    x_ref, own_ref, peer_ref, base_ref, amp_ref, q_ref, k_ref, out_ref, acc, tab, emb,
):
    count = x_ref.shape[0]

    @pl.when(pl.program_id(0) == 0)
    def _():
        acc[...] = jnp.zeros_like(acc)
        cols = jnp.transpose(own_ref[...] + peer_ref[...])
        mean = cols[:, 0:1] / width
        rstd = lax.rsqrt(cols[:, 1:2] / width - mean * mean + 1e-06)
        tab[0] = jnp.broadcast_to(mean, (count, size))
        tab[1] = jnp.broadcast_to(rstd, (count, size))
        t_now = steps_ref[level_ref[0]].astype(F32)
        first = lax.axis_index("tp") * (width // lax.axis_size("tp"))
        emb[...] = time_embed(t_now, lax.broadcasted_iota(jnp.int32, emb.shape, 1) + first)

    for h in range(heads):
        cut = slice(h * size, (h + 1) * size)
        off = (h * size) % PERIOD
        mod = lambda i: base_ref[i, :, cut] + amp_ref[i, :, cut] * emb[0:1, off : off + size]
        x = x_ref[:, cut].astype(F32)
        mixed = normed_mix(x, tab[0], tab[1], mod(0), mod(1))
        both = jnp.concatenate([q_ref[0, h], k_ref[0, h]], axis=1)
        raw = jnp.dot(mixed, both, preferred_element_type=F32)
        acc[...] += raw * raw

    @pl.when(pl.program_id(0) == pl.num_programs(0) - 1)
    def _():
        fill = lambda i: jnp.full((count, 1), steps_ref[level_ref[0] + i].astype(F32))
        out_ref[...] = to_rows(
            [
                tab[0][:, 0:1],
                tab[1][:, 0:1],
                jnp.sum(acc[:, :size], axis=1, keepdims=True),
                jnp.sum(acc[:, size:], axis=1, keepdims=True),
                fill(0),
                fill(1),
            ],
            size,
        )


def token_squares(x, own, peer, levels, steps_table, base, amp, q_weight, k_weight, width):
    count = x.shape[0]
    local_heads, size = q_weight.shape[1], q_weight.shape[2]
    heads = divisor(local_heads, SUM_HEADS)
    tokens = pl.BlockSpec((count, heads * size), lambda i, *_: (0, i))
    modspec = pl.BlockSpec((base.shape[0], 1, heads * size), lambda i, *_: (0, 0, i))
    weight = pl.BlockSpec((1, heads, size, size), lambda i, *_: (0, i, 0, 0))
    return pl.pallas_call(
        functools.partial(squares_kernel, heads, size, width),
        name="token_squares",
        grid_spec=pltpu.PrefetchScalarGridSpec(
            num_scalar_prefetch=2,
            grid=(local_heads // heads,),
            in_specs=[tokens, VMEM, VMEM, modspec, modspec, weight, weight],
            out_specs=pl.BlockSpec((8, count), lambda i, *_: (0, 0)),
            scratch_shapes=[
                pltpu.VMEM((count, 2 * size), F32),
                pltpu.VMEM((2, count, size), F32),
                pltpu.VMEM((8, PERIOD), F32),
            ],
        ),
        out_shape=jax.ShapeDtypeStruct((8, count), F32),
        compiler_params=pltpu.CompilerParams(dimension_semantics=("arbitrary",), vmem_limit_bytes=LIMIT),
        cost_estimate=pl.CostEstimate(
            flops=4 * count * local_heads * size * size,
            bytes_accessed=2 * count * local_heads * size + 4 * local_heads * size * size,
            transcendentals=0,
        ),
    )(levels, steps_table, x, own, peer, base, amp, q_weight, k_weight)


def tables_kernel(
    first, pos_ref, a_ref, b_ref, c_ref, d_ref,
    mean_ref, rstd_ref, ck_ref, sk_ref, cq_ref, sq_ref, emb_ref, step_ref,
):
    count, size = mean_ref.shape[1:]
    frames = -(-count // HW_DEV)
    position = lax.axis_index("queue")
    last = lax.axis_size("queue") - 1
    inner = lax.broadcasted_iota(jnp.int32, (HW_DEV, size), 0)
    part, freq = pair_plan((HW_DEV, size), size)
    hpos = (inner // WIDE).astype(F32)
    wpos = (inner % WIDE).astype(F32)
    angle = jnp.where(part == 1, hpos, wpos) * freq
    pcos, psin = jnp.cos(angle), jnp.sin(angle)
    row = lax.broadcasted_iota(jnp.int32, (8, size), 0)
    _, ffreq = pair_plan((8, size), size)
    sign = jnp.where(lax.broadcasted_iota(jnp.int32, (1, size), 1) < size // 2, -1.0, 1.0)
    emb_row = lax.broadcasted_iota(jnp.int32, emb_ref.shape, 0)
    moment = jnp.zeros(emb_ref.shape, F32)
    for g, stats in enumerate((a_ref, b_ref, c_ref, d_ref)):
        start = pos_ref[jnp.clip(position + (g - 2), 0, last)]
        fangle = (start + row).astype(F32) * ffreq
        fcos, fsin = jnp.cos(fangle), jnp.sin(fangle)
        cols = jnp.transpose(stats[...])
        moment = jnp.where(emb_row == g, stats[4:5, 0:1], moment)
        for f in range(frames):
            lo, hi = f * HW_DEV, min((f + 1) * HW_DEV, count)
            cos = jnp.where(part == 0, fcos[f : f + 1], pcos)[: hi - lo]
            sin = jnp.where(part == 0, fsin[f : f + 1], psin)[: hi - lo] * sign
            column = lambda j: jnp.broadcast_to(cols[lo:hi, j : j + 1], (hi - lo, size))
            mean_ref[g, lo:hi] = column(0)
            rstd_ref[g, lo:hi] = column(1)
            ck_ref[g, lo:hi] = cos * column(3)
            sk_ref[g, lo:hi] = sin * column(3)
            if g in (1, 2):
                cq_ref[g - 1, lo:hi] = cos * column(2)
                sq_ref[g - 1, lo:hi] = sin * column(2)
    channel = lax.broadcasted_iota(jnp.int32, emb_ref.shape, 1) + lax.axis_index("tp") * first
    emb_ref[...] = time_embed(moment, channel)
    step_ref[...] = jnp.broadcast_to((b_ref[5:6, 0:size] - b_ref[4:5, 0:size]) / 1000.0, step_ref.shape)


def tables(stats, group_pos, first, count, size):
    four = jax.ShapeDtypeStruct((4, count, size), F32)
    two = jax.ShapeDtypeStruct((2, count, size), F32)
    return pl.pallas_call(
        functools.partial(tables_kernel, first),
        name="token_tables",
        in_specs=[pl.BlockSpec(memory_space=pltpu.SMEM)] + [VMEM] * 4,
        out_specs=[VMEM] * 8,
        out_shape=[four, four, four, four, two, two]
        + [jax.ShapeDtypeStruct((8, PERIOD), F32), jax.ShapeDtypeStruct((8, size), F32)],
        compiler_params=pltpu.CompilerParams(vmem_limit_bytes=LIMIT),
        cost_estimate=pl.CostEstimate(flops=count * size * 60, bytes_accessed=count * size * 80, transcendentals=0),
    )(group_pos, *stats)


def attend_kernel(
    heads, size,
    a_ref, near_ref, own_ref, far_ref, base_ref, amp_ref, q_ref, k_ref, v_ref,
    mean_ref, rstd_ref, ck_ref, sk_ref, cq_ref, sq_ref, emb_ref, step_ref, *rest,
):
    vel_ref, new_ref = rest[-2:]
    count = own_ref.shape[0]
    position = lax.axis_index("queue")
    odd = position % 2 == 1
    has_a, has_b, has_d = position > 1, position > 0, position < lax.axis_size("queue") - 1
    for h in range(heads):
        cut = slice(h * size, (h + 1) * size)
        start = pl.multiple_of((pl.program_id(0) * heads + h) * size, size)
        off = (h * size) % PERIOD
        near, far = near_ref[:, pl.ds(start, size)].astype(F32), far_ref[:, pl.ds(start, size)].astype(F32)
        x = [
            a_ref[:, pl.ds(start, size)].astype(F32),
            jnp.where(odd, near, far),
            own_ref[:, cut].astype(F32),
            jnp.where(odd, far, near),
        ]
        mod = lambda g, i: base_ref[i, :, cut] + amp_ref[i, :, cut] * emb_ref[g : g + 1, off : off + size]
        mixed = jnp.concatenate(
            [normed_mix(x[g], mean_ref[g], rstd_ref[g], mod(g, 0), mod(g, 1)) for g in range(4)], axis=0
        )
        both = jnp.concatenate([k_ref[h], v_ref[0, h]], axis=1)
        raw_kv = jnp.dot(mixed, both, preferred_element_type=F32)
        raw_q = jnp.dot(mixed[count : 3 * count], q_ref[h], preferred_element_type=F32)
        part = lambda raw, g: raw[g * count : (g + 1) * count]

        def turned(raw, cos, sin):
            return (raw * cos + pltpu.roll(raw, size // 2, 1) * sin).astype(BF16)

        key = [turned(part(raw_kv, g)[:, :size], ck_ref[g], sk_ref[g]) for g in range(4)]
        query = [turned(part(raw_q, g), cq_ref[g], sq_ref[g]) for g in range(2)]
        value = [part(raw_kv, g)[:, size:].astype(BF16) for g in range(4)]
        ones = [jnp.ones((count, size), BF16)] * 4
        for g, there in ((0, has_a), (1, has_b), (3, has_d)):
            key[g] = jnp.where(there, key[g], key[2])
            value[g] = jnp.where(there, value[g], jnp.zeros_like(value[g]))
            ones[g] = jnp.where(there, ones[g], jnp.zeros_like(ones[g]))
        outs = []
        for g in range(2):
            keys = jnp.concatenate(key[g : g + 3], axis=0)
            wide = jnp.concatenate(
                [jnp.concatenate(value[g : g + 3], axis=0), jnp.concatenate(ones[g : g + 3], axis=0)],
                axis=1,
            )
            scores = lax.dot_general(
                query[g], keys, (((1,), (1,)), ((), ())), preferred_element_type=F32
            )
            top = jnp.max(scores, axis=-1, keepdims=True)
            weights = jnp.exp2(scores - top).astype(BF16)
            total = jnp.dot(weights, wide, preferred_element_type=F32)
            outs.append(total[:, :size] / total[:, size:])
        state = x[2] + mod(2, 2) * outs[1]
        vel_ref[:, cut] = state.astype(BF16)
        state = x[1] + mod(1, 2) * outs[0]
        moved = x[1] + step_ref[0:1, :] * state
        new_ref[:, cut] = jnp.where(has_b, moved, 0.0).astype(BF16)


def attend(lo, hi, a, near, own, far, base, amp, q, k, v, tabs, sofar):
    count = own.shape[0]
    size = v.shape[2]
    heads = divisor(math.gcd(lo, hi - lo), STEP_HEADS)
    first = lo // heads
    whole = pl.BlockSpec((count, heads * size), lambda i: (0, i + first))
    modspec = pl.BlockSpec((base.shape[0], 1, heads * size), lambda i: (0, 0, i + first))
    single = pl.BlockSpec((heads, size, size), lambda i: (i + first, 0, 0))
    lone = pl.BlockSpec((1, heads, size, size), lambda i: (0, i + first, 0, 0))
    keys = 3 * count
    number = hi - lo
    ins = [VMEM, VMEM, whole, VMEM, modspec, modspec, single, single, lone] + [VMEM] * len(tabs)
    return pl.pallas_call(
        functools.partial(attend_kernel, heads, size),
        name="attend_heads",
        grid=(number // heads,),
        in_specs=ins + [pl.BlockSpec(memory_space=pl.ANY)] * len(sofar),
        out_specs=[whole] * 2,
        out_shape=[jax.ShapeDtypeStruct(own.shape, BF16)] * 2,
        input_output_aliases={len(ins) + i: i for i in range(len(sofar))},
        compiler_params=pltpu.CompilerParams(dimension_semantics=("arbitrary",), vmem_limit_bytes=LIMIT),
        cost_estimate=pl.CostEstimate(
            flops=number * (20 * count * size * size + 8 * count * keys * size),
            bytes_accessed=12 * count * number * size + 10 * number * size * size,
            transcendentals=2 * number * count * keys,
        ),
    )(a, near, own, far, base, amp, q, k, v, *tabs, *sofar)


def body(hidden, q_weight, k_weight, v_weight, mod_base, mod_amp, levels, steps_table, group_pos):
    count, local_width = hidden.shape
    local_heads, size = q_weight.shape[1], q_weight.shape[2]
    length = lax.axis_size("queue")
    width = local_width * lax.axis_size("tp")
    everyone = range(length)
    base = mod_base[0][:, None, :]
    amp = mod_amp[0][:, None, :]

    cuts = [2 * (local_heads // 2 * i // CHUNKS) for i in range(CHUNKS)] + [local_heads]
    *pieces, sums = split(hidden, cuts, size)
    near, back, far = [], [], []
    for piece in pieces:
        near.append(send(piece, [(i, i ^ 1) for i in everyone], length))
        back.append(send(piece, [(i, i + 2) for i in everyone], length))
    for piece in near:
        far.append(send(piece, [(i, i - 2 if i % 2 else i + 2) for i in everyone], length))

    peer = other_core(sums)
    squares = token_squares(hidden, sums, peer, levels, steps_table, base, amp, q_weight, k_weight, width)
    total = squares + other_core(squares)
    line = jnp.arange(8, dtype=jnp.int32)[:, None]
    factor = jnp.where(line == 2, math.log2(math.e) / math.sqrt(size), 1.0)
    own_stats = jnp.where((line == 2) | (line == 3), lax.rsqrt(total / width + 1e-06) * factor, squares)
    stats = [
        send(own_stats, [(i, i + 2) for i in everyone], length, wrap=True),
        send(own_stats, [(i, i + 1) for i in everyone], length, wrap=True),
        own_stats,
        send(own_stats, [(i, i - 1) for i in everyone], length, wrap=True),
    ]
    tabs = tables(stats, group_pos, local_width, count, size)
    apart = pairs_apart(size)
    q = jnp.einsum("hde,ef->hdf", q_weight[0], apart)
    k = jnp.einsum("hde,ef->hdf", k_weight[0], apart)

    outs = ()
    for c, (lo, hi) in enumerate(zip(cuts[:-1], cuts[1:])):
        outs = attend(lo, hi, back[c], near[c], hidden, far[c], base, amp, q, k, v_weight, tabs, outs)
    velocity, new_queue = outs
    return (new_queue, velocity)


def solution(mesh):
    return jax.shard_map(
        body,
        mesh=mesh,
        in_specs=(
            P(("groups", "queue"), "tp"),
            P(None, "tp", None, None),
            P(None, "tp", None, None),
            P(None, "tp", None, None),
            P(None, None, "tp"),
            P(None, None, "tp"),
            P(("groups", "queue")),
            P(),
            P("groups"),
        ),
        out_specs=(P(("groups", "queue"), "tp"), P(("groups", "queue"), "tp")),
        check_vma=False,
    )
```

profile of v0, /device:TPU:0, one launch (start us, length us, event | category | flops | bytes accessed | tf_op | source)
XLA Modules:
  0.0 79.1 jit_solution(14296620660407229656)
XLA Ops:
  0.6 0.0 copy-start
  0.6 1.2 %copy-done = bf16[208,2560]{1,0:T(8,128)(2,1)S(1)} copy-done((bf16[208,2560]{1,0:T(8,128)(2,1)S(1)}, bf16[208,2560]{1,0:T(8,128)(2,1)}, u32[]{:S(2)}) %copy-start) | copy-done | bytes 1064984
  1.9 0.0 copy-start.2
  1.9 0.0 copy-start.5
  1.9 0.0 copy-start.6
  1.9 0.0 copy-start.7
  1.9 0.5 token_split.1
  2.4 3.0 %collective-permute-start.9 = (bf16[208,1280]{1,0:T(8,128)(2,1)S(1)}, bf16[208,1280]{1,0:T(8,128)(2,1)S(1)}, u32[]{:S(2)}, u32[]{:S(2)}) collective-permute-start(bf16[208,1280]{1,0:T(8,128)(2,1)S(1)} %get-tuple-element.27), channel_id=1, source_target_pairs={{0,2},{2,0},{4,6},{6,4},{8,10},{10,8},{12,14},{14,12},{1,3},{3,1},... | collective-permute-start | bytes 1597448 | tf_op jit(solution)/shard_map/ppermute | solution.py:27
  5.4 0.1 collective-permute-start.1
  5.5 4.0 %collective-permute-start = (bf16[208,1280]{1,0:T(8,128)(2,1)S(1)}, bf16[208,1280]{1,0:T(8,128)(2,1)S(1)}, u32[]{:S(2)}, u32[]{:S(2)}) collective-permute-start(bf16[208,1280]{1,0:T(8,128)(2,1)S(1)} %get-tuple-element.17), channel_id=1, source_target_pairs={{0,4},{2,6},{4,8},{6,10},{8,12},{10,14},{1,5},{3,7},{5,9},{7,11},{... | collective-permute-start | bytes 1597448 | tf_op jit(solution)/shard_map/ppermute | solution.py:27
  9.5 3.5 %collective-permute-start.8 = (bf16[208,1280]{1,0:T(8,128)(2,1)S(1)}, bf16[208,1280]{1,0:T(8,128)(2,1)S(1)}, u32[]{:S(2)}, u32[]{:S(2)}) collective-permute-start(bf16[208,1280]{1,0:T(8,128)(2,1)S(1)} %get-tuple-element.27), channel_id=1, source_target_pairs={{0,4},{2,6},{4,8},{6,10},{8,12},{10,14},{1,5},{3,7},{5,9},{7,11},{... | collective-permute-start | bytes 1597448 | tf_op jit(solution)/shard_map/ppermute | solution.py:27
  12.9 0.1 collective-permute-start.3
  13.7 0.5 collective-permute-done.3.peer_ref
  14.2 0.0 copy-done.2
  14.2 0.0 copy-done.5
  14.2 0.0 copy-done.6
  14.2 0.0 copy-done.7
  14.2 0.0 copy-start.3
  14.2 1.1 %copy-done.3 = bf16[1,20,128,128]{3,2,1,0:T(8,128)(2,1)S(1)} copy-done((bf16[1,20,128,128]{3,2,1,0:T(8,128)(2,1)S(1)}, bf16[1,20,128,128]{3,2,1,0:T(8,128)(2,1)}, u32[]{:S(2)}) %copy-start.3) | copy-done | bytes 655384
  15.3 2.7 %token_squares.1 = f32[8,208]{1,0:T(8,128)S(1)} custom-call(s32[1]{0:T(128)S(6)} %copy.19.level_ref, s32[65]{0:T(128)S(1)} %copy-done.7, bf16[208,2560]{1,0:T(8,128)(2,1)S(1)} %copy-done, f32[8,208]{1,0:T(8,128)S(1)} %get-tuple-element.18.own_ref, f32[8,208]{1,0:T(8,128)S(1)} %collective-permute-done.3.peer_ref, f32[3,1,2560]{2,1,0:T(1,128)S(1)} %bitcast.16, ...), custom_call_target="tpu_custom_call" | custom-call | flops 272629760 | bytes 2375680 | tf_op jit(solution)/shard_map/token_squares/pallas_call | solution.py:160
  18.0 0.2 collective-permute-start.4
  18.2 1.0 %collective-permute-done.4 = f32[8,208]{1,0:T(8,128)S(1)} collective-permute-done((f32[8,208]{1,0:T(8,128)S(1)}, f32[8,208]{1,0:T(8,128)S(1)}, u32[]{:S(2)}, u32[]{:S(2)}) %collective-permute-start.4) | collective-permute-done | bytes 6688 | tf_op jit(solution)/shard_map/ppermute | solution.py:32
  19.3 0.1 multiply_select_fusion.c_ref
  19.3 0.1 collective-permute-start.7
  19.4 0.0 collective-permute-done.9.near_ref
  19.4 4.8 %collective-permute-start.10 = (bf16[208,1280]{1,0:T(8,128)(2,1)S(1)}, bf16[208,1280]{1,0:T(8,128)(2,1)S(1)}, u32[]{:S(2)}, u32[]{:S(2)}) collective-permute-start(bf16[208,1280]{1,0:T(8,128)(2,1)S(1)} %collective-permute-done.9.near_ref), channel_id=1, source_target_pairs={{0,4},{4,8},{6,2},{8,12},{10,6},{14,10},{1,5},{5,9},{7,3},{9,13},{... | collective-permute-start | bytes 1597448 | tf_op jit(solution)/shard_map/ppermute | solution.py:27
  24.2 0.0 copy-start.8
  24.2 0.0 copy-start.1
  24.2 0.0 copy-start.4
  24.3 9.2 %collective-permute-done.7.d_ref = f32[8,208]{1,0:T(8,128)S(1)} collective-permute-done((f32[8,208]{1,0:T(8,128)S(1)}, f32[8,208]{1,0:T(8,128)S(1)}, u32[]{:S(2)}, u32[]{:S(2)}) %collective-permute-start.7) | collective-permute-done | bytes 6688 | tf_op jit(solution)/shard_map/ppermute | solution.py:27
  33.5 0.0 collective-permute-start.6
  33.5 0.0 collective-permute-done.1.near_ref
  33.5 1.3 %collective-permute-start.2 = (bf16[208,1280]{1,0:T(8,128)(2,1)S(1)}, bf16[208,1280]{1,0:T(8,128)(2,1)S(1)}, u32[]{:S(2)}, u32[]{:S(2)}) collective-permute-start(bf16[208,1280]{1,0:T(8,128)(2,1)S(1)} %collective-permute-done.1.near_ref), channel_id=1, source_target_pairs={{0,4},{4,8},{6,2},{8,12},{10,6},{14,10},{1,5},{5,9},{7,3},{9,13},{... | collective-permute-start | bytes 1597448 | tf_op jit(solution)/shard_map/ppermute | solution.py:27
  34.8 0.4 convolution_bitcast_fusion.k_ref
  35.2 5.2 %collective-permute-done.6.b_ref = f32[8,208]{1,0:T(8,128)S(1)} collective-permute-done((f32[8,208]{1,0:T(8,128)S(1)}, f32[8,208]{1,0:T(8,128)S(1)}, u32[]{:S(2)}, u32[]{:S(2)}) %collective-permute-start.6) | collective-permute-done | bytes 6688 | tf_op jit(solution)/shard_map/ppermute | solution.py:27
  40.4 0.0 collective-permute-start.5
  40.4 0.4 convolution_bitcast_fusion.1.q_ref
  40.8 14.0 %collective-permute-done.5.a_ref = f32[8,208]{1,0:T(8,128)S(1)} collective-permute-done((f32[8,208]{1,0:T(8,128)S(1)}, f32[8,208]{1,0:T(8,128)S(1)}, u32[]{:S(2)}, u32[]{:S(2)}) %collective-permute-start.5) | collective-permute-done | bytes 6688 | tf_op jit(solution)/shard_map/ppermute | solution.py:27
  54.8 0.0 copy-done.8
  54.8 1.3 %token_tables.1 = (f32[4,208,128]{2,1,0:T(8,128)S(1)}, f32[4,208,128]{2,1,0:T(8,128)S(1)}, f32[4,208,128]{2,1,0:T(8,128)S(1)}, f32[4,208,128]{2,1,0:T(8,128)S(1)...) custom-call(s32[8]{0:T(128)S(1)} %copy-done.8, ...), custom_call_target="tpu_custom_call" | custom-call | flops 1597440 | bytes 2129920 | tf_op jit(solution)/shard_map/token_tables/pallas_call | solution.py:229
  56.0 0.0 collective-permute-done.8.a_ref
  56.1 0.0 collective-permute-done.10.far_ref
  56.1 0.0 copy-done.1
  56.1 0.0 copy-done.4
  56.1 11.5 %attend_heads.2 = (bf16[208,2560]{1,0:T(8,128)(2,1)}, bf16[208,2560]{1,0:T(8,128)(2,1)}) custom-call(bf16[208,1280]{1,0:T(8,128)(2,1)S(1)} %collective-permute-done.8.a_ref, bf16[208,1280]{1,0:T(8,128)(2,1)S(1)} %collective-permute-done.9.near_ref, bf16[208,2560]{1,0:T(8,128)(2,1)S(1)} %copy-done.1, bf16[208,1280]{1,0:T(8,128)(2,1)S(1)} %collective-permute-done.10.far_ref, ...), custom_call_target="tpu_custom_call" | custom-call | flops 2010644480 | bytes 4833280 | tf_op jit(solution)/shard_map/attend_heads/pallas_call | solution.py:315
  67.6 0.0 collective-permute-done.a_ref
  67.6 0.0 collective-permute-done.2.far_ref
  67.6 11.5 %attend_heads.3 = (bf16[208,2560]{1,0:T(8,128)(2,1)}, bf16[208,2560]{1,0:T(8,128)(2,1)}) custom-call(bf16[208,1280]{1,0:T(8,128)(2,1)S(1)} %collective-permute-done.a_ref, bf16[208,1280]{1,0:T(8,128)(2,1)S(1)} %collective-permute-done.1.near_ref, bf16[208,2560]{1,0:T(8,128)(2,1)S(1)} %copy-done.1, ...), custom_call_target="tpu_custom_call", output_to_operand_aliasing={{0}: (17, {}), {1}: (18, {})} | custom-call | flops 2010644480 | bytes 4833280 | tf_op jit(solution)/shard_map/attend_heads/pallas_call | solution.py:315
  (3 shorter events, 0.0 us)
Async XLA Ops:
  0.6 1.2 %copy-start = (bf16[208,2560]{1,0:T(8,128)(2,1)S(1)}, bf16[208,2560]{1,0:T(8,128)(2,1)}, u32[]{:S(2)}) copy-start(bf16[208,2560]{1,0:T(8,128)(2,1)} %own_ref.3) | copy-start | bytes 3194884
  1.9 12.3 %copy-start.2 = (bf16[1,20,128,128]{3,2,1,0:T(8,128)(2,1)S(1)}, bf16[1,20,128,128]{3,2,1,0:T(8,128)(2,1)}, u32[]{:S(2)}) copy-start(bf16[1,20,128,128]{3,2,1,0:T(8,128)(2,1)} %k_ref.1) | copy-start | bytes 1966084
  1.9 12.3 %copy-start.5 = (f32[1,3,2560]{2,0,1:T(1,128)S(1)}, f32[1,3,2560]{2,0,1:T(1,128)}, u32[]{:S(2)}) copy-start(f32[1,3,2560]{2,0,1:T(1,128)} %param.13) | copy-start | bytes 92164
  1.9 12.3 %copy-start.6 = (f32[1,3,2560]{2,0,1:T(1,128)S(1)}, f32[1,3,2560]{2,0,1:T(1,128)}, u32[]{:S(2)}) copy-start(f32[1,3,2560]{2,0,1:T(1,128)} %param.14) | copy-start | bytes 92164
  1.9 12.3 %copy-start.7 = (s32[65]{0:T(128)S(1)}, s32[65]{0:T(128)}, u32[]{:S(2)}) copy-start(s32[65]{0:T(128)} %steps_ref.1) | copy-start | bytes 784
  2.4 17.0 %collective-permute-start.9 = (bf16[208,1280]{1,0:T(8,128)(2,1)S(1)}, bf16[208,1280]{1,0:T(8,128)(2,1)S(1)}, u32[]{:S(2)}, u32[]{:S(2)}) collective-permute-start(bf16[208,1280]{1,0:T(8,128)(2,1)S(1)} %get-tuple-element.27), channel_id=1, source_target_pairs={{0,2},{2,0},{4,6},{6,4},{8,10},{10,8},{12,14},{14,12},{1,3},{3,1},... | collective-permute-start | bytes 1597448 | tf_op jit(solution)/shard_map/ppermute | solution.py:27
  5.4 28.1 %collective-permute-start.1 = (bf16[208,1280]{1,0:T(8,128)(2,1)S(1)}, bf16[208,1280]{1,0:T(8,128)(2,1)S(1)}, u32[]{:S(2)}, u32[]{:S(2)}) collective-permute-start(bf16[208,1280]{1,0:T(8,128)(2,1)S(1)} %get-tuple-element.17), channel_id=1, source_target_pairs={{0,2},{2,0},{4,6},{6,4},{8,10},{10,8},{12,14},{14,12},{1,3},{3,1},... | collective-permute-start | bytes 1597448 | tf_op jit(solution)/shard_map/ppermute | solution.py:27
  5.5 62.1 %collective-permute-start = (bf16[208,1280]{1,0:T(8,128)(2,1)S(1)}, bf16[208,1280]{1,0:T(8,128)(2,1)S(1)}, u32[]{:S(2)}, u32[]{:S(2)}) collective-permute-start(bf16[208,1280]{1,0:T(8,128)(2,1)S(1)} %get-tuple-element.17), channel_id=1, source_target_pairs={{0,4},{2,6},{4,8},{6,10},{8,12},{10,14},{1,5},{3,7},{5,9},{7,11},{... | collective-permute-start | bytes 1597448 | tf_op jit(solution)/shard_map/ppermute | solution.py:27
  9.5 46.6 %collective-permute-start.8 = (bf16[208,1280]{1,0:T(8,128)(2,1)S(1)}, bf16[208,1280]{1,0:T(8,128)(2,1)S(1)}, u32[]{:S(2)}, u32[]{:S(2)}) collective-permute-start(bf16[208,1280]{1,0:T(8,128)(2,1)S(1)} %get-tuple-element.27), channel_id=1, source_target_pairs={{0,4},{2,6},{4,8},{6,10},{8,12},{10,14},{1,5},{3,7},{5,9},{7,11},{... | collective-permute-start | bytes 1597448 | tf_op jit(solution)/shard_map/ppermute | solution.py:27
  12.9 1.2 %collective-permute-start.3 = (f32[8,208]{1,0:T(8,128)S(1)}, f32[8,208]{1,0:T(8,128)S(1)}, u32[]{:S(2)}, u32[]{:S(2)}) collective-permute-start(f32[8,208]{1,0:T(8,128)S(1)} %get-tuple-element.18.own_ref), channel_id=1, source_target_pairs={{0,1},{1,0},{2,3},{3,2},{4,5},{5,4},{6,7},{7,6},{8,9},{9,8},{10,11... | collective-permute-start | bytes 19976 | tf_op jit(solution)/shard_map/ppermute | solution.py:32
  14.2 1.1 %copy-start.3 = (bf16[1,20,128,128]{3,2,1,0:T(8,128)(2,1)S(1)}, bf16[1,20,128,128]{3,2,1,0:T(8,128)(2,1)}, u32[]{:S(2)}) copy-start(bf16[1,20,128,128]{3,2,1,0:T(8,128)(2,1)} %q_ref.1) | copy-start | bytes 1966084
  18.0 1.2 %collective-permute-start.4 = (f32[8,208]{1,0:T(8,128)S(1)}, f32[8,208]{1,0:T(8,128)S(1)}, u32[]{:S(2)}, u32[]{:S(2)}) collective-permute-start(f32[8,208]{1,0:T(8,128)S(1)} %token_squares.1), channel_id=1, source_target_pairs={{0,1},{1,0},{2,3},{3,2},{4,5},{5,4},{6,7},{7,6},{8,9},{9,8},{10,11... | collective-permute-start | bytes 19976 | tf_op jit(solution)/shard_map/ppermute | solution.py:32
  19.3 14.2 %collective-permute-start.7 = (f32[8,208]{1,0:T(8,128)S(1)}, f32[8,208]{1,0:T(8,128)S(1)}, u32[]{:S(2)}, u32[]{:S(2)}) collective-permute-start(f32[8,208]{1,0:T(8,128)S(1)} %multiply_select_fusion.c_ref), channel_id=1, source_target_pairs={{0,14},{2,0},{4,2},{6,4},{8,6},{10,8},{12,10},{14,12},{1,15},{3,1}... | collective-permute-start | bytes 19976 | tf_op jit(solution)/shard_map/ppermute | solution.py:27
  19.4 36.6 %collective-permute-start.10 = (bf16[208,1280]{1,0:T(8,128)(2,1)S(1)}, bf16[208,1280]{1,0:T(8,128)(2,1)S(1)}, u32[]{:S(2)}, u32[]{:S(2)}) collective-permute-start(bf16[208,1280]{1,0:T(8,128)(2,1)S(1)} %collective-permute-done.9.near_ref), channel_id=1, source_target_pairs={{0,4},{4,8},{6,2},{8,12},{10,6},{14,10},{1,5},{5,9},{7,3},{9,13},{... | collective-permute-start | bytes 1597448 | tf_op jit(solution)/shard_map/ppermute | solution.py:27
  24.2 30.6 %copy-start.8 = (s32[8]{0:T(128)S(1)}, s32[8]{0:T(128)}, u32[]{:S(2)}) copy-start(s32[8]{0:T(128)} %pos_ref.1) | copy-start | bytes 100
  24.2 31.8 %copy-start.1 = (bf16[208,2560]{1,0:T(8,128)(2,1)S(1)}, bf16[208,2560]{1,0:T(8,128)(2,1)}, u32[]{:S(2)}) copy-start(bf16[208,2560]{1,0:T(8,128)(2,1)} %own_ref.3) | copy-start | bytes 3194884
  24.2 31.8 %copy-start.4 = (bf16[1,20,128,128]{3,2,1,0:T(8,128)(2,1)S(1)}, bf16[1,20,128,128]{3,2,1,0:T(8,128)(2,1)}, u32[]{:S(2)}) copy-start(bf16[1,20,128,128]{3,2,1,0:T(8,128)(2,1)} %v_ref.3) | copy-start | bytes 1966084
  33.5 6.9 %collective-permute-start.6 = (f32[8,208]{1,0:T(8,128)S(1)}, f32[8,208]{1,0:T(8,128)S(1)}, u32[]{:S(2)}, u32[]{:S(2)}) collective-permute-start(f32[8,208]{1,0:T(8,128)S(1)} %multiply_select_fusion.c_ref), channel_id=1, source_target_pairs={{0,2},{2,4},{4,6},{6,8},{8,10},{10,12},{12,14},{14,0},{1,3},{3,5},... | collective-permute-start | bytes 19976 | tf_op jit(solution)/shard_map/ppermute | solution.py:27
  33.5 34.1 %collective-permute-start.2 = (bf16[208,1280]{1,0:T(8,128)(2,1)S(1)}, bf16[208,1280]{1,0:T(8,128)(2,1)S(1)}, u32[]{:S(2)}, u32[]{:S(2)}) collective-permute-start(bf16[208,1280]{1,0:T(8,128)(2,1)S(1)} %collective-permute-done.1.near_ref), channel_id=1, source_target_pairs={{0,4},{4,8},{6,2},{8,12},{10,6},{14,10},{1,5},{5,9},{7,3},{9,13},{... | collective-permute-start | bytes 1597448 | tf_op jit(solution)/shard_map/ppermute | solution.py:27
  40.4 14.4 %collective-permute-start.5 = (f32[8,208]{1,0:T(8,128)S(1)}, f32[8,208]{1,0:T(8,128)S(1)}, u32[]{:S(2)}, u32[]{:S(2)}) collective-permute-start(f32[8,208]{1,0:T(8,128)S(1)} %multiply_select_fusion.c_ref), channel_id=1, source_target_pairs={{0,4},{2,6},{4,8},{6,10},{8,12},{10,14},{12,0},{14,2},{1,5},{3,7},... | collective-permute-start | bytes 19976 | tf_op jit(solution)/shard_map/ppermute | solution.py:27
where the time goes:
time: 79.3 us; the launch traced here: 79.1 us
  waiting for transfers between devices  29.9 us (38%)
  Pallas kernels  27.5 us (35%)
  starting transfers between devices  17 us (21%)
  local copies, waits for them, and re-layouts  2.34 us (3%)
  between operations  1.45 us (2%)
  matrix products  0.8 us (1%)
    ppermute x9, waiting for transfers between devices, send(): return lax.ppermute(array, 'queue', pairs)  28.4 us
    pallas_call x2, Pallas kernels, attend(): pl.pallas_call(functools.partial(attend_kernel, heads, size), name='atten...  23 us
    ppermute x9, starting transfers between devices, send(): return lax.ppermute(array, 'queue', pairs)  16.7 us
    pallas_call x1, Pallas kernels, token_squares(): pl.pallas_call(functools.partial(squares_kernel, heads, size, width), nam...  2.73 us
    unnamed x18, local copies, waits for them, and re-layouts  2.34 us
  transfers between devices with their start and end apart: 11, of which 5 were waited for; matrix products, arithmetic and copies ran while one was open for 1% of the time, Pallas kernels for 20%

commit v1 on v0

v1 whole, which is shorter than its diff:
```python
import functools
import math

import jax
import jax.numpy as jnp
from jax import lax
from jax.experimental import pallas as pl
from jax.experimental.pallas import tpu as pltpu
from jax.sharding import PartitionSpec as P

WIDE = 52
HW_DEV = 104
PERIOD = 256
CHUNKS = 2
SUM_HEADS = 5
LIMIT = 24 << 20
F32 = jnp.float32
BF16 = jnp.bfloat16
VMEM = pl.BlockSpec(memory_space=pltpu.VMEM)
HBM = pl.BlockSpec(memory_space=pltpu.HBM)


def send(array, pairs, length, wrap=False):
    if wrap:
        pairs = [(a, b % length) for a, b in pairs]
    pairs = [(a, b) for a, b in pairs if 0 <= b < length]
    return lax.ppermute(array, "queue", pairs)


def other_core(array):
    if lax.axis_size("tp") == 2:
        return lax.ppermute(array, "tp", [(0, 1), (1, 0)])
    return lax.psum(array, "tp") - array


def in_hbm(array):
    return pltpu.with_memory_space_constraint(array, pltpu.HBM)


def divisor(count, most):
    return max(k for k in range(1, most + 1) if count % k == 0)


def time_embed(moment, channel):
    within = channel % 256
    freq = jnp.exp(-jnp.log(10000.0) * (within % 128).astype(F32) / 128.0)
    angle = moment * freq
    return jnp.where(within < 128, jnp.cos(angle), jnp.sin(angle))


def pair_plan(shape, size):
    half = size // 2
    side = size // 6
    lead = (size - 4 * side) // 2
    pair = lax.broadcasted_iota(jnp.int32, shape, len(shape) - 1) % half
    part = jnp.where(pair < lead, 0, jnp.where(pair < lead + side, 1, 2))
    within = pair - jnp.where(part == 0, 0, jnp.where(part == 1, lead, lead + side))
    pairs = jnp.where(part == 0, lead, side).astype(F32)
    return part, jnp.exp(-math.log(10000.0) * (within.astype(F32) / pairs))


def block_maps(weight, apart):
    heads, size = weight.shape[:2]
    col = jnp.arange(2 * size)[None, :]
    half = size // 2
    if apart:
        source = 2 * (col % half) + col // size
        owner = col % size // half
    else:
        source = col % size
        owner = col // size
    spread = (jnp.arange(size)[:, None] == source).astype(BF16)
    full = jnp.einsum("pde,ef->pdf", weight.reshape(heads // 2, 2 * size, size), spread)
    mine = jnp.arange(2 * size)[:, None] // size == owner
    return jnp.where(mine, full, jnp.zeros_like(full))


def normed_mix(x, mean, rstd, shift, scale):
    return ((x - mean) * rstd * (1.0 + scale) + shift).astype(BF16)


def to_rows(columns, size):
    count = columns[0].shape[0]
    lane = lax.broadcasted_iota(jnp.int32, (count, size), 1)
    wide = jnp.zeros((count, size), F32)
    for j, column in enumerate(columns):
        wide = jnp.where(lane == j, jnp.broadcast_to(column, (count, size)), wide)
    return jnp.transpose(wide)[:8]


def split_kernel(size, cuts, x_hbm, *refs):
    outs, (x_ref, sums_ref, sems) = refs[: len(cuts) - 1], refs[len(cuts) - 1 :]
    count, _ = x_ref.shape
    blocks = []
    for piece, lo, hi in zip(outs, cuts[:-1], cuts[1:]):
        middle = (lo + hi) // 2
        for start, stop in ((lo, middle), (middle, hi)):
            here = slice(start * size, stop * size)
            there = slice((start - lo) * size, (stop - lo) * size)
            i = len(blocks)
            blocks.append(
                (
                    start,
                    stop,
                    pltpu.make_async_copy(x_hbm.at[:, here], x_ref.at[:, here], sems.at[0, i]),
                    pltpu.make_async_copy(x_ref.at[:, here], piece.at[:, there], sems.at[1, i]),
                )
            )
    for *_, come, _ in blocks:
        come.start()
    total = jnp.zeros((count, size), F32)
    second = jnp.zeros((count, size), F32)
    for start, stop, come, go in blocks:
        come.wait()
        go.start()
        for h in range(start, stop):
            x = x_ref[:, h * size : (h + 1) * size].astype(F32)
            total += x
            second += x * x
    sums_ref[...] = to_rows(
        [jnp.sum(total, axis=1, keepdims=True), jnp.sum(second, axis=1, keepdims=True)], size
    )
    for *_, go in blocks:
        go.wait()


def split(x, cuts, size):
    count, width = x.shape
    return pl.pallas_call(
        functools.partial(split_kernel, size, cuts),
        name="token_split",
        in_specs=[HBM],
        out_specs=[HBM] * (len(cuts) - 1) + [VMEM, VMEM],
        out_shape=[jax.ShapeDtypeStruct((count, (hi - lo) * size), BF16) for lo, hi in zip(cuts[:-1], cuts[1:])]
        + [jax.ShapeDtypeStruct(x.shape, BF16), jax.ShapeDtypeStruct((8, count), F32)],
        scratch_shapes=[pltpu.SemaphoreType.DMA((2, 2 * len(cuts) - 2))],
        compiler_params=pltpu.CompilerParams(vmem_limit_bytes=LIMIT),
        cost_estimate=pl.CostEstimate(flops=4 * count * width, bytes_accessed=4 * count * width, transcendentals=0),
    )(in_hbm(x))


def squares_kernel(
    width, level_ref, steps_hbm, x_ref, own_ref, peer_ref, base_hbm, amp_hbm, q_hbm, k_hbm,
    out_ref, acc, tab, emb, steps, base, amp, q_ref, k_ref, sems,
):
    count = x_ref.shape[0]
    local_heads, size = q_ref.shape[:2]
    share = divisor(local_heads, SUM_HEADS)
    small = [
        pltpu.make_async_copy(src, dst, sems.at[i])
        for i, (src, dst) in enumerate(((steps_hbm, steps), (base_hbm, base), (amp_hbm, amp)))
    ]
    large = [
        [
            pltpu.make_async_copy(
                src.at[0, lo : lo + share], dst.at[lo : lo + share], sems.at[3 + 2 * (lo // share) + i]
            )
            for i, (src, dst) in enumerate(((q_hbm, q_ref), (k_hbm, k_ref)))
        ]
        for lo in range(0, local_heads, share)
    ]
    for copy in small + sum(large, []):
        copy.start()
    acc[...] = jnp.zeros_like(acc)
    cols = jnp.transpose(own_ref[...] + peer_ref[...])
    mean = cols[:, 0:1] / width
    rstd = lax.rsqrt(cols[:, 1:2] / width - mean * mean + 1e-06)
    tab[0] = jnp.broadcast_to(mean, (count, size))
    tab[1] = jnp.broadcast_to(rstd, (count, size))
    for copy in small:
        copy.wait()
    moment = [steps[level_ref[0] + i].astype(F32) for i in range(2)]
    first = lax.axis_index("tp") * (width // lax.axis_size("tp"))
    emb[...] = time_embed(moment[0], lax.broadcasted_iota(jnp.int32, emb.shape, 1) + first)
    for h in range(local_heads):
        if h % share == 0:
            for copy in large[h // share]:
                copy.wait()
        cut = slice(h * size, (h + 1) * size)
        off = (h * size) % PERIOD
        mod = lambda i: base[i, :, cut] + amp[i, :, cut] * emb[0:1, off : off + size]
        mixed = normed_mix(x_ref[:, cut].astype(F32), tab[0], tab[1], mod(0), mod(1))
        both = jnp.concatenate([q_ref[h], k_ref[h]], axis=1)
        raw = jnp.dot(mixed, both, preferred_element_type=F32)
        acc[...] += raw * raw
    out_ref[...] = to_rows(
        [
            mean,
            rstd,
            jnp.sum(acc[:, :size], axis=1, keepdims=True),
            jnp.sum(acc[:, size:], axis=1, keepdims=True),
            jnp.full((count, 1), moment[0]),
            jnp.full((count, 1), moment[1]),
        ],
        size,
    )


def token_squares(x, own, peer, levels, steps_table, base, amp, q_weight, k_weight, width):
    count = x.shape[0]
    local_heads, size = q_weight.shape[1], q_weight.shape[2]
    number = local_heads // divisor(local_heads, SUM_HEADS)
    return pl.pallas_call(
        functools.partial(squares_kernel, width),
        name="token_squares",
        in_specs=[pl.BlockSpec(memory_space=pltpu.SMEM), HBM, VMEM, VMEM, VMEM] + [HBM] * 4,
        out_specs=VMEM,
        out_shape=jax.ShapeDtypeStruct((8, count), F32),
        scratch_shapes=[
            pltpu.VMEM((count, 2 * size), F32),
            pltpu.VMEM((2, count, size), F32),
            pltpu.VMEM((8, PERIOD), F32),
            pltpu.SMEM(steps_table.shape, jnp.int32),
            pltpu.VMEM(base.shape, F32),
            pltpu.VMEM(amp.shape, F32),
            pltpu.VMEM(q_weight.shape[1:], BF16),
            pltpu.VMEM(k_weight.shape[1:], BF16),
            pltpu.SemaphoreType.DMA((3 + 2 * number,)),
        ],
        compiler_params=pltpu.CompilerParams(vmem_limit_bytes=LIMIT),
        cost_estimate=pl.CostEstimate(
            flops=4 * count * local_heads * size * size,
            bytes_accessed=2 * count * local_heads * size + 4 * local_heads * size * size,
            transcendentals=0,
        ),
    )(levels, in_hbm(steps_table), x, own, peer, *map(in_hbm, (base, amp, q_weight, k_weight)))


def tables_kernel(
    first, pos_ref, a_ref, b_ref, c_ref, d_ref,
    mean_ref, rstd_ref, ck_ref, sk_ref, cq_ref, sq_ref, emb_ref, step_ref,
):
    count, size = mean_ref.shape[1:]
    frames = -(-count // HW_DEV)
    position = lax.axis_index("queue")
    last = lax.axis_size("queue") - 1
    inner = lax.broadcasted_iota(jnp.int32, (HW_DEV, size), 0)
    part, freq = pair_plan((HW_DEV, size), size)
    hpos = (inner // WIDE).astype(F32)
    wpos = (inner % WIDE).astype(F32)
    angle = jnp.where(part == 1, hpos, wpos) * freq
    pcos, psin = jnp.cos(angle), jnp.sin(angle)
    row = lax.broadcasted_iota(jnp.int32, (8, size), 0)
    _, ffreq = pair_plan((8, size), size)
    emb_row = lax.broadcasted_iota(jnp.int32, emb_ref.shape, 0)
    moment = jnp.zeros(emb_ref.shape, F32)
    for g, stats in enumerate((a_ref, b_ref, c_ref, d_ref)):
        start = pos_ref[jnp.clip(position + (g - 2), 0, last)]
        fangle = (start + row).astype(F32) * ffreq
        fcos, fsin = jnp.cos(fangle), jnp.sin(fangle)
        cols = jnp.transpose(stats[...])
        moment = jnp.where(emb_row == g, stats[4:5, 0:1], moment)
        for f in range(frames):
            lo, hi = f * HW_DEV, min((f + 1) * HW_DEV, count)
            cos = jnp.where(part == 0, fcos[f : f + 1], pcos)[: hi - lo]
            sin = jnp.where(part == 0, fsin[f : f + 1], psin)[: hi - lo]
            column = lambda j: jnp.broadcast_to(cols[lo:hi, j : j + 1], (hi - lo, size))
            mean_ref[g, lo:hi] = column(0)
            rstd_ref[g, lo:hi] = column(1)
            ck_ref[g, lo:hi] = cos * column(3)
            sk_ref[g, lo:hi] = sin * column(3)
            if g in (1, 2):
                cq_ref[g - 1, lo:hi] = cos * column(2)
                sq_ref[g - 1, lo:hi] = sin * column(2)
    channel = lax.broadcasted_iota(jnp.int32, emb_ref.shape, 1) + lax.axis_index("tp") * first
    emb_ref[...] = time_embed(moment, channel)
    step_ref[...] = jnp.broadcast_to((b_ref[5:6, 0:size] - b_ref[4:5, 0:size]) / 1000.0, step_ref.shape)


def tables(stats, group_pos, first, count, size):
    four = jax.ShapeDtypeStruct((4, count, size), F32)
    two = jax.ShapeDtypeStruct((2, count, size), F32)
    return pl.pallas_call(
        functools.partial(tables_kernel, first),
        name="token_tables",
        in_specs=[pl.BlockSpec(memory_space=pltpu.SMEM)] + [VMEM] * 4,
        out_specs=[VMEM] * 8,
        out_shape=[four, four, four, four, two, two]
        + [jax.ShapeDtypeStruct((8, PERIOD), F32), jax.ShapeDtypeStruct((8, size), F32)],
        compiler_params=pltpu.CompilerParams(vmem_limit_bytes=LIMIT),
        cost_estimate=pl.CostEstimate(flops=count * size * 60, bytes_accessed=count * size * 80, transcendentals=0),
    )(group_pos, *stats)


def attend_kernel(
    lo, number, size, relayed,
    near_ref, own_ref, ahead_ref, across_ref, base_ref, amp_ref, q_ref, k_ref, v_ref,
    mean_ref, rstd_ref, ck_ref, sk_ref, cq_ref, sq_ref, emb_ref, step_ref, *rest,
):
    vel_hbm, new_hbm, keys, wide, queries, vel_out, new_out, sems = rest[-8:]
    count = own_ref.shape[0]
    two = 2 * size
    first = lo // 2
    position = lax.axis_index("queue")
    odd = position % 2 == 1
    has_b = position > 0
    there = {0: position > 1, 1: has_b, 3: position < lax.axis_size("queue") - 1}
    rows = lambda g: slice(g * count, (g + 1) * count)
    half = (slice(0, size), slice(size, two))

    def lanes(pair, side):
        return pl.ds(pl.multiple_of(pair * two + side * size, size), size)

    def tokens(pair, side, g):
        held = lambda ref: ref[:, lanes(pair, side)]
        if g == 2:
            return own_ref[:, lanes(first + pair, side)].astype(F32)
        if g == 0:
            back = held(ahead_ref)
            if relayed:
                back = jnp.where(odd, back, held(rest[0]))
            return back.astype(F32)
        near, far = held(near_ref), held(across_ref)
        if relayed:
            far = jnp.where(odd, far, held(rest[1]))
        return (jnp.where(odd, near, far) if g == 1 else jnp.where(odd, far, near)).astype(F32)

    def mod(pair, side, g, i):
        off = (side * size) % PERIOD
        cut = lanes(first + pair, side)
        return base_ref[i, :, cut] + amp_ref[i, :, cut] * emb_ref[g : g + 1, off : off + size]

    def mix(pair, g):
        return jnp.concatenate(
            [
                normed_mix(
                    tokens(pair, side, g), mean_ref[g], rstd_ref[g], mod(pair, side, g, 0), mod(pair, side, g, 1)
                )
                for side in range(2)
            ],
            axis=1,
        )

    def turned(raw, cos, sin):
        one, other = raw[:, :size], raw[:, size:]
        return (one * cos - other * sin).astype(BF16), (one * sin + other * cos).astype(BF16)

    def project(pair, slot, g, mixed):
        key = turned(jnp.dot(mixed, k_ref[first + pair], preferred_element_type=F32), ck_ref[g], sk_ref[g])
        raw = jnp.dot(mixed, v_ref[first + pair], preferred_element_type=F32).astype(BF16)
        for i in range(2):
            value = raw[:, half[i]]
            part = key[i]
            if g in there:
                part = jnp.where(there[g], part, keys[slot, rows(2), half[i]])
                value = jnp.where(there[g], value, jnp.zeros_like(value))
            keys[slot, rows(g), half[i]] = part
            wide[slot, i, rows(g), :size] = value
        if g in (1, 2):
            raw = jnp.dot(mixed, q_ref[first + pair], preferred_element_type=F32)
            parts = turned(raw, cq_ref[g - 1], sq_ref[g - 1])
            lane = lax.broadcasted_iota(jnp.int32, (1, size), 1)
            for side in range(2):
                mine = (lane < size // 2) == (side == 0)
                for i in range(2):
                    queries[slot, g - 1, rows(side), half[i]] = jnp.where(mine, parts[i], jnp.zeros_like(parts[i]))

    def score(slot, g):
        return lax.dot_general(
            queries[slot, g],
            keys[slot, g * count : (g + 3) * count],
            (((1,), (1,)), ((), ())),
            preferred_element_type=F32,
        )

    def soften(scores):
        top = jnp.max(scores, axis=-1, keepdims=True)
        return jnp.exp2(scores - top).astype(BF16)

    def gather(slot, side, g, weights):
        total = jnp.dot(weights, wide[slot, side, g * count : (g + 3) * count], preferred_element_type=F32)
        return total[:, :size] / total[:, size:]

    def finish(pair, slot, side, g, attn):
        x = tokens(pair, side, g + 1)
        state = x + mod(pair, side, g + 1, 2) * attn
        if g == 1:
            vel_out[slot, :, half[side]] = state.astype(BF16)
        else:
            moved = x + step_ref[0:1, :] * state
            new_out[slot, :, half[side]] = jnp.where(has_b, moved, 0.0).astype(BF16)

    def copies(pair, slot):
        to = pl.ds(pl.multiple_of((first + pair) * two, two), two)
        return [
            pltpu.make_async_copy(out.at[slot], hbm.at[:, to], sems.at[i, slot])
            for i, (out, hbm) in enumerate(((vel_out, vel_hbm), (new_out, new_hbm)))
        ]

    def attention(pair, slot, following):
        other = 1 - slot
        if isinstance(pair, int):
            if pair >= 2:
                for copy in copies(pair - 2, slot):
                    copy.wait()
        else:
            @pl.when(pair >= 2)
            def _():
                for copy in copies(pair - 2, slot):
                    copy.wait()

        for g, groups in ((0, (2, 1)), (1, (0, 3))):
            scores = score(slot, g)
            if following:
                mixed = [mix(pair + 1, j) for j in groups]
            weights = soften(scores[rows(0)])
            if following:
                project(pair + 1, other, groups[0], mixed[0])
            total = gather(slot, 0, g, weights)
            weights = soften(scores[rows(1)])
            finish(pair, slot, 0, g, total)
            if following:
                project(pair + 1, other, groups[1], mixed[1])
            total = gather(slot, 1, g, weights)
            finish(pair, slot, 1, g, total)
        for copy in copies(pair, slot):
            copy.start()

    pairs = number // 2
    for g in range(4):
        ones = jnp.ones((count, size), BF16)
        if g in there:
            ones = jnp.where(there[g], ones, jnp.zeros_like(ones))
        for slot in range(2):
            for side in range(2):
                wide[slot, side, rows(g), size:] = ones
    for g in (2, 1, 0, 3):
        project(0, 0, g, mix(0, g))
    looped = (pairs - 1) // 2

    def step(i, _):
        attention(2 * i, 0, True)
        attention(2 * i + 1, 1, True)

    lax.fori_loop(0, looped, step, None)
    for pair in range(2 * looped, pairs):
        attention(pair, pair % 2, pair < pairs - 1)
    for pair in range(max(0, pairs - 2), pairs):
        for copy in copies(pair, pair % 2):
            copy.wait()


def attend(lo, hi, near, own, ahead, across, relay, base, amp, q, k, v, tabs, sofar):
    count = own.shape[0]
    size = v.shape[2] // 2
    keys = 3 * count
    number = hi - lo
    hbm = pl.BlockSpec(memory_space=pl.ANY)
    ins = [VMEM] * (9 + len(tabs) + len(relay))
    return pl.pallas_call(
        functools.partial(attend_kernel, lo, number, size, bool(relay)),
        name="attend_heads",
        in_specs=ins + [hbm] * len(sofar),
        out_specs=[hbm] * 2,
        out_shape=[jax.ShapeDtypeStruct(own.shape, BF16)] * 2,
        scratch_shapes=[
            pltpu.VMEM((2, 4 * count, 2 * size), BF16),
            pltpu.VMEM((2, 2, 4 * count, 2 * size), BF16),
            pltpu.VMEM((2, 2, 2 * count, 2 * size), BF16),
            pltpu.VMEM((2, count, 2 * size), BF16),
            pltpu.VMEM((2, count, 2 * size), BF16),
            pltpu.SemaphoreType.DMA((2, 2)),
        ],
        input_output_aliases={len(ins) + i: i for i in range(len(sofar))},
        compiler_params=pltpu.CompilerParams(vmem_limit_bytes=LIMIT),
        cost_estimate=pl.CostEstimate(
            flops=number * (20 * count * size * size + 8 * count * keys * size),
            bytes_accessed=12 * count * number * size + 10 * number * size * size,
            transcendentals=2 * number * count * keys,
        ),
    )(near, own, ahead, across, base, amp, q, k, v, *tabs, *relay, *sofar)


def body(hidden, q_weight, k_weight, v_weight, mod_base, mod_amp, levels, steps_table, group_pos):
    count, local_width = hidden.shape
    local_heads, size = q_weight.shape[1], q_weight.shape[2]
    length = lax.axis_size("queue")
    width = local_width * lax.axis_size("tp")
    everyone = range(length)
    base = mod_base[0][:, None, :]
    amp = mod_amp[0][:, None, :]

    cuts = [2 * (local_heads // 2 * i // CHUNKS) for i in range(CHUNKS)] + [local_heads]
    *pieces, rows, sums = split(hidden, cuts, size)
    swap = [(i, i ^ 1) for i in everyone]
    two_on = [(i, i + 2) for i in everyone]
    both_ways = [(i, i - 2 if i % 2 else i + 2) for i in everyone]
    near, ahead, across, more = [], [], [], []
    for c, piece in enumerate(pieces):
        near.append(send(piece, swap, length))
        if c < CHUNKS - 1 or length % 2:
            ahead.append(send(piece, two_on, length))
            across.append(send(near[c], both_ways, length))
            more.append(())
        else:
            ahead.append(send(piece, two_on[1::2], length))
            across.append(send(near[c], both_ways[1::2], length))
            even = send(piece, two_on[0::2], length)
            more.append((even, send(ahead[c], swap, length)))

    peer = other_core(sums)
    squares = token_squares(rows, sums, peer, levels, steps_table, base, amp, q_weight, k_weight, width)
    total = squares + other_core(squares)
    line = jnp.arange(8, dtype=jnp.int32)[:, None]
    factor = jnp.where(line == 2, math.log2(math.e) / math.sqrt(size), 1.0)
    own_stats = jnp.where((line == 2) | (line == 3), lax.rsqrt(total / width + 1e-06) * factor, squares)
    stats = [
        send(own_stats, [(i, i + 2) for i in everyone], length, wrap=True),
        send(own_stats, [(i, i + 1) for i in everyone], length, wrap=True),
        own_stats,
        send(own_stats, [(i, i - 1) for i in everyone], length, wrap=True),
    ]
    tabs = tables(stats, group_pos, local_width, count, size)
    q = block_maps(q_weight[0], True)
    k = block_maps(k_weight[0], True)
    v = block_maps(v_weight[0], False)

    outs = ()
    for c, (lo, hi) in enumerate(zip(cuts[:-1], cuts[1:])):
        outs = attend(lo, hi, near[c], rows, ahead[c], across[c], more[c], base, amp, q, k, v, tabs, outs)
    velocity, new_queue = outs
    return (new_queue, velocity)


def solution(mesh):
    return jax.shard_map(
        body,
        mesh=mesh,
        in_specs=(
            P(("groups", "queue"), "tp"),
            P(None, "tp", None, None),
            P(None, "tp", None, None),
            P(None, "tp", None, None),
            P(None, None, "tp"),
            P(None, None, "tp"),
            P(("groups", "queue")),
            P(),
            P("groups"),
        ),
        out_specs=(P(("groups", "queue"), "tp"), P(("groups", "queue"), "tp")),
        check_vma=False,
    )
```

time: 79.3 us -> 78.8 us (level)
  starting transfers between devices: 17 us -> 21.9 us
  Pallas kernels: 27.5 us -> 23.6 us
  local copies, waits for them, and re-layouts: 2.34 us -> 0.04 us
  matrix products: 0.8 us -> 1.72 us
    pallas_call x3, Pallas kernels: 25.7 us -> 20.7 us  [the longest x2 18.1 us: attend(): pl.pallas_call(functools.partial(attend_kernel, lo, number, size, bool(re...]
    ppermute x9 -> x11, starting transfers between devices: 16.7 us -> 21.7 us  [send(): return lax.ppermute(array, 'queue', pairs)]
    unnamed x18 -> x12, local copies, waits for them, and re-layouts: 2.34 us -> 0.04 us
    pallas_call x1, Pallas kernels: 0.54 us -> 1.66 us  [split(): pl.pallas_call(functools.partial(split_kernel, size, cuts), name='token_s...]
    dot_general x2 -> x3, matrix products: 0.8 us -> 1.72 us  [block_maps(): jnp.einsum('pde,ef->pdf', weight.reshape(heads // 2, 2 * size, size), spr...]
    ppermute x9 -> x11, waiting for transfers between devices: 28.4 us -> 28.2 us  [send(): return lax.ppermute(array, 'queue', pairs)]
  transfers between devices with their start and end apart: 11 -> 13, of which waited for: 5 -> 6; matrix products, arithmetic and copies ran while one was open for 1% -> 2% of each run, Pallas kernels for 20% -> 16%
where the time goes in v1:
time: 78.8 us; the launch traced here: 78.6 us
  waiting for transfers between devices  29.3 us (37%)
  Pallas kernels  23.6 us (30%)
  starting transfers between devices  21.9 us (28%)
  matrix products  1.72 us (2%)
  between operations  1.71 us (2%)
    ppermute x11, waiting for transfers between devices, send(): return lax.ppermute(array, 'queue', pairs)  28.2 us
    ppermute x11, starting transfers between devices, send(): return lax.ppermute(array, 'queue', pairs)  21.7 us
    pallas_call x2, Pallas kernels, attend(): pl.pallas_call(functools.partial(attend_kernel, lo, number, size, bool(re...  18.1 us
    pallas_call x1, Pallas kernels, token_squares(): pl.pallas_call(functools.partial(squares_kernel, width), name='token_squa...  2.61 us
    dot_general x3, matrix products, block_maps(): jnp.einsum('pde,ef->pdf', weight.reshape(heads // 2, 2 * size, size), spr...  1.72 us
    pallas_call x1, Pallas kernels, split(): pl.pallas_call(functools.partial(split_kernel, size, cuts), name='token_s...  1.66 us
  transfers between devices with their start and end apart: 13, of which 6 were waited for; matrix products, arithmetic and copies ran while one was open for 2% of the time, Pallas kernels for 16%

profile of v1, /device:TPU:0, one launch (start us, length us, event | category | flops | bytes accessed | tf_op | source)
XLA Modules:
  0.0 78.6 jit_solution(14596160262319163709)
XLA Ops:
  0.6 0.0 copy-start
  0.6 1.7 %token_split.1 = (bf16[208,1280]{1,0:T(8,128)(2,1)S(1)}, bf16[208,1280]{1,0:T(8,128)(2,1)S(1)}, bf16[208,2560]{1,0:T(8,128)(2,1)S(1)}, f32[8,208]{1,0:T(8,128)S(1)}) custom-call(bf16[208,2560]{1,0:T(8,128)(2,1)} %x_hbm.1), custom_call_target="tpu_custom_call" | custom-call | flops 2129920 | bytes 2129920 | tf_op jit(solution)/shard_map/token_split/pallas_call | solution.py:129
  2.3 0.7 collective-permute-start.1
  3.0 5.9 %collective-permute-start = (bf16[208,1280]{1,0:T(8,128)(2,1)S(1)}, bf16[208,1280]{1,0:T(8,128)(2,1)S(1)}, u32[]{:S(2)}, u32[]{:S(2)}) collective-permute-start(bf16[208,1280]{1,0:T(8,128)(2,1)S(1)} %get-tuple-element.18), channel_id=1, source_target_pairs={{0,2},{2,0},{4,6},{6,4},{8,10},{10,8},{12,14},{14,12},{1,3},{3,1},... | collective-permute-start | bytes 1597448 | tf_op jit(solution)/shard_map/ppermute | solution.py:27
  8.9 0.0 collective-permute-start.3
  8.9 0.2 collective-permute-start.10
  9.0 0.0 copy-start.4
  9.0 0.1 broadcast_compare_fusion
  9.9 0.1 collective-permute-done.3.peer_ref
  10.0 2.6 %token_squares.1 = f32[8,208]{1,0:T(8,128)S(1)} custom-call(s32[1]{0:T(128)S(6)} %copy.21.level_ref, s32[65]{0:T(128)} %steps_hbm.1, bf16[208,2560]{1,0:T(8,128)(2,1)S(1)} %get-tuple-element.19.x_ref.own_ref, f32[8,208]{1,0:T(8,128)S(1)} %get-tuple-element.20.own_ref, f32[8,208]{1,0:T(8,128)S(1)} %collective-permute-done.3.peer_ref, f32[3,1,2560]{2,1,0:T(1,128)} %bitcast.28, ...), custom_call_target="tpu_custom_call" | custom-call | flops 272629760 | bytes 2375680 | tf_op jit(solution)/shard_map/token_squares/pallas_call | solution.py:203
  12.7 0.0 copy-start.5
  12.7 0.3 collective-permute-start.4
  13.0 0.9 %collective-permute-done.4 = f32[8,208]{1,0:T(8,128)S(1)} collective-permute-done((f32[8,208]{1,0:T(8,128)S(1)}, f32[8,208]{1,0:T(8,128)S(1)}, u32[]{:S(2)}, u32[]{:S(2)}) %collective-permute-start.4) | collective-permute-done | bytes 6688 | tf_op jit(solution)/shard_map/ppermute | solution.py:32
  13.9 0.1 multiply_select_fusion.c_ref
  14.0 2.6 %collective-permute-start.7 = (f32[8,208]{1,0:T(8,128)S(1)}, f32[8,208]{1,0:T(8,128)S(1)}, u32[]{:S(2)}, u32[]{:S(2)}) collective-permute-start(f32[8,208]{1,0:T(8,128)S(1)} %multiply_select_fusion.c_ref), channel_id=1, source_target_pairs={{0,14},{2,0},{4,2},{6,4},{8,6},{10,8},{12,10},{14,12},{1,15},{3,1}... | collective-permute-start | bytes 19976 | tf_op jit(solution)/shard_map/ppermute | solution.py:27
  16.5 0.0 collective-permute-start.6
  16.5 0.0 copy-done.4
  16.5 0.6 fusion.1.k_ref
  17.1 15.3 %collective-permute-done.7.d_ref = f32[8,208]{1,0:T(8,128)S(1)} collective-permute-done((f32[8,208]{1,0:T(8,128)S(1)}, f32[8,208]{1,0:T(8,128)S(1)}, u32[]{:S(2)}, u32[]{:S(2)}) %collective-permute-start.7) | collective-permute-done | bytes 6688 | tf_op jit(solution)/shard_map/ppermute | solution.py:27
  32.4 3.5 %collective-permute-start.11 = (bf16[208,1280]{1,0:T(8,128)(2,1)S(1)}, bf16[208,1280]{1,0:T(8,128)(2,1)S(1)}, u32[]{:S(2)}, u32[]{:S(2)}) collective-permute-start(bf16[208,1280]{1,0:T(8,128)(2,1)S(1)} %get-tuple-element.29), channel_id=1, source_target_pairs={{0,4},{2,6},{4,8},{6,10},{8,12},{10,14},{1,5},{3,7},{5,9},{7,11},{... | collective-permute-start | bytes 1597448 | tf_op jit(solution)/shard_map/ppermute | solution.py:27
  35.9 0.0 collective-permute-done.6.b_ref
  35.9 1.6 %collective-permute-start.5 = (f32[8,208]{1,0:T(8,128)S(1)}, f32[8,208]{1,0:T(8,128)S(1)}, u32[]{:S(2)}, u32[]{:S(2)}) collective-permute-start(f32[8,208]{1,0:T(8,128)S(1)} %multiply_select_fusion.c_ref), channel_id=1, source_target_pairs={{0,4},{2,6},{4,8},{6,10},{8,12},{10,14},{12,0},{14,2},{1,5},{3,7},... | collective-permute-start | bytes 19976 | tf_op jit(solution)/shard_map/ppermute | solution.py:27
  37.5 0.0 collective-permute-done.10.near_ref
  37.5 2.0 %collective-permute-start.12 = (bf16[208,1280]{1,0:T(8,128)(2,1)S(1)}, bf16[208,1280]{1,0:T(8,128)(2,1)S(1)}, u32[]{:S(2)}, u32[]{:S(2)}) collective-permute-start(bf16[208,1280]{1,0:T(8,128)(2,1)S(1)} %collective-permute-done.10.near_ref), channel_id=1, source_target_pairs={{0,4},{4,8},{6,2},{8,12},{10,6},{14,10},{1,5},{5,9},{7,3},{9,13},{... | collective-permute-start | bytes 1597448 | tf_op jit(solution)/shard_map/ppermute | solution.py:27
  39.5 0.0 copy-done.5
  39.5 0.6 fusion.2.q_ref
  40.1 0.0 copy-start.3
  40.1 0.0 copy-start.1
  40.1 0.0 copy-start.2
  40.1 8.4 %collective-permute-done.5.a_ref = f32[8,208]{1,0:T(8,128)S(1)} collective-permute-done((f32[8,208]{1,0:T(8,128)S(1)}, f32[8,208]{1,0:T(8,128)S(1)}, u32[]{:S(2)}, u32[]{:S(2)}) %collective-permute-start.5) | collective-permute-done | bytes 6688 | tf_op jit(solution)/shard_map/ppermute | solution.py:27
  48.5 4.4 %collective-permute-start.8 = (bf16[208,1280]{1,0:T(8,128)(2,1)S(1)}, bf16[208,1280]{1,0:T(8,128)(2,1)S(1)}, u32[]{:S(2)}, u32[]{:S(2)}) collective-permute-start(bf16[208,1280]{1,0:T(8,128)(2,1)S(1)} %get-tuple-element.18), channel_id=1, source_target_pairs={{0,4},{4,8},{8,12},{1,5},{5,9},{9,13},{16,20},{20,24},{24,28},{17,... | collective-permute-start | bytes 1597448 | tf_op jit(solution)/shard_map/ppermute | solution.py:27
  53.0 0.0 collective-permute-done.1.ahead_ref
  53.0 0.1 collective-permute-start.9
  53.0 0.0 collective-permute-done.near_ref
  53.1 0.9 %collective-permute-start.2 = (bf16[208,1280]{1,0:T(8,128)(2,1)S(1)}, bf16[208,1280]{1,0:T(8,128)(2,1)S(1)}, u32[]{:S(2)}, u32[]{:S(2)}) collective-permute-start(bf16[208,1280]{1,0:T(8,128)(2,1)S(1)} %collective-permute-done.near_ref), channel_id=1, source_target_pairs={{6,2},{10,6},{14,10},{7,3},{11,7},{15,11},{22,18},{26,22},{30,26},... | collective-permute-start | bytes 1597448 | tf_op jit(solution)/shard_map/ppermute | solution.py:27
  53.9 0.0 copy-done
  54.0 0.6 fusion.v_ref
  54.5 0.0 copy-done.3
  54.6 1.3 %token_tables.1 = (f32[4,208,128]{2,1,0:T(8,128)S(1)}, f32[4,208,128]{2,1,0:T(8,128)S(1)}, f32[4,208,128]{2,1,0:T(8,128)S(1)}, f32[4,208,128]{2,1,0:T(8,128)S(1)...) custom-call(s32[8]{0:T(128)S(1)} %copy-done.3, ...), custom_call_target="tpu_custom_call" | custom-call | flops 1597440 | bytes 2129920 | tf_op jit(solution)/shard_map/token_tables/pallas_call | solution.py:273
  55.8 0.0 collective-permute-done.11.ahead_ref
  55.8 4.1 %collective-permute-done.12.across_ref = bf16[208,1280]{1,0:T(8,128)(2,1)S(1)} collective-permute-done((bf16[208,1280]{1,0:T(8,128)(2,1)S(1)}, bf16[208,1280]{1,0:T(8,128)(2,1)S(1)}, u32[]{:S(2)}, u32[]{:S(2)}) %collective-permute-start.12) | collective-permute-done | bytes 532512 | tf_op jit(solution)/shard_map/ppermute | solution.py:27
  60.0 0.0 copy-done.1
  60.0 0.0 copy-done.2
  60.0 9.0 %attend_heads.2 = (bf16[208,2560]{1,0:T(8,128)(2,1)}, bf16[208,2560]{1,0:T(8,128)(2,1)}) custom-call(bf16[208,1280]{1,0:T(8,128)(2,1)S(1)} %collective-permute-done.10.near_ref, bf16[208,2560]{1,0:T(8,128)(2,1)S(1)} %get-tuple-element.19.x_ref.own_ref, bf16[208,1280]{1,0:T(8,128)(2,1)S(1)} %collective-permute-done.11.ahead_ref, ...), custom_call_target="tpu_custom_call" | custom-call | flops 2010644480 | bytes 4833280 | tf_op jit(solution)/shard_map/attend_heads/pallas_call | solution.py:450
  69.0 0.4 collective-permute-done.8.rest_0_
  69.4 0.0 collective-permute-done.9.rest_1_
  69.4 0.0 collective-permute-done.2.across_ref
  69.4 9.0 %attend_heads.3 = (bf16[208,2560]{1,0:T(8,128)(2,1)}, bf16[208,2560]{1,0:T(8,128)(2,1)}) custom-call(bf16[208,1280]{1,0:T(8,128)(2,1)S(1)} %collective-permute-done.near_ref, bf16[208,2560]{1,0:T(8,128)(2,1)S(1)} %get-tuple-element.19.x_ref.own_ref, ...), custom_call_target="tpu_custom_call", output_to_operand_aliasing={{0}: (19, {}), {1}: (20, {})} | custom-call | flops 2010644480 | bytes 4833280 | tf_op jit(solution)/shard_map/attend_heads/pallas_call | solution.py:450
  (5 shorter events, 0.0 us)
Async XLA Ops:
  0.6 53.3 %copy-start = (bf16[1,20,128,128]{3,2,1,0:T(8,128)(2,1)S(1)}, bf16[1,20,128,128]{3,2,1,0:T(8,128)(2,1)}, u32[]{:S(2)}) copy-start(bf16[1,20,128,128]{3,2,1,0:T(8,128)(2,1)} %param.12) | copy-start | bytes 1966084
  2.3 50.6 %collective-permute-start.1 = (bf16[208,1280]{1,0:T(8,128)(2,1)S(1)}, bf16[208,1280]{1,0:T(8,128)(2,1)S(1)}, u32[]{:S(2)}, u32[]{:S(2)}) collective-permute-start(bf16[208,1280]{1,0:T(8,128)(2,1)S(1)} %get-tuple-element.18), channel_id=1, source_target_pairs={{2,6},{6,10},{10,14},{3,7},{7,11},{11,15},{18,22},{22,26},{26,30},... | collective-permute-start | bytes 1597448 | tf_op jit(solution)/shard_map/ppermute | solution.py:27
  3.0 50.0 %collective-permute-start = (bf16[208,1280]{1,0:T(8,128)(2,1)S(1)}, bf16[208,1280]{1,0:T(8,128)(2,1)S(1)}, u32[]{:S(2)}, u32[]{:S(2)}) collective-permute-start(bf16[208,1280]{1,0:T(8,128)(2,1)S(1)} %get-tuple-element.18), channel_id=1, source_target_pairs={{0,2},{2,0},{4,6},{6,4},{8,10},{10,8},{12,14},{14,12},{1,3},{3,1},... | collective-permute-start | bytes 1597448 | tf_op jit(solution)/shard_map/ppermute | solution.py:27
  8.9 1.2 %collective-permute-start.3 = (f32[8,208]{1,0:T(8,128)S(1)}, f32[8,208]{1,0:T(8,128)S(1)}, u32[]{:S(2)}, u32[]{:S(2)}) collective-permute-start(f32[8,208]{1,0:T(8,128)S(1)} %get-tuple-element.20.own_ref), channel_id=1, source_target_pairs={{0,1},{1,0},{2,3},{3,2},{4,5},{5,4},{6,7},{7,6},{8,9},{9,8},{10,11... | collective-permute-start | bytes 19976 | tf_op jit(solution)/shard_map/ppermute | solution.py:32
  8.9 28.7 %collective-permute-start.10 = (bf16[208,1280]{1,0:T(8,128)(2,1)S(1)}, bf16[208,1280]{1,0:T(8,128)(2,1)S(1)}, u32[]{:S(2)}, u32[]{:S(2)}) collective-permute-start(bf16[208,1280]{1,0:T(8,128)(2,1)S(1)} %get-tuple-element.29), channel_id=1, source_target_pairs={{0,2},{2,0},{4,6},{6,4},{8,10},{10,8},{12,14},{14,12},{1,3},{3,1},... | collective-permute-start | bytes 1597448 | tf_op jit(solution)/shard_map/ppermute | solution.py:27
  9.0 7.5 %copy-start.4 = (bf16[1,20,128,128]{3,2,1,0:T(8,128)(2,1)S(1)}, bf16[1,20,128,128]{3,2,1,0:T(8,128)(2,1)}, u32[]{:S(2)}) copy-start(bf16[1,20,128,128]{3,2,1,0:T(8,128)(2,1)} %k_hbm.1) | copy-start | bytes 1966084
  12.7 26.9 %copy-start.5 = (bf16[1,20,128,128]{3,2,1,0:T(8,128)(2,1)S(1)}, bf16[1,20,128,128]{3,2,1,0:T(8,128)(2,1)}, u32[]{:S(2)}) copy-start(bf16[1,20,128,128]{3,2,1,0:T(8,128)(2,1)} %q_hbm.1) | copy-start | bytes 1966084
  12.7 1.2 %collective-permute-start.4 = (f32[8,208]{1,0:T(8,128)S(1)}, f32[8,208]{1,0:T(8,128)S(1)}, u32[]{:S(2)}, u32[]{:S(2)}) collective-permute-start(f32[8,208]{1,0:T(8,128)S(1)} %token_squares.1), channel_id=1, source_target_pairs={{0,1},{1,0},{2,3},{3,2},{4,5},{5,4},{6,7},{7,6},{8,9},{9,8},{10,11... | collective-permute-start | bytes 19976 | tf_op jit(solution)/shard_map/ppermute | solution.py:32
  14.0 18.5 %collective-permute-start.7 = (f32[8,208]{1,0:T(8,128)S(1)}, f32[8,208]{1,0:T(8,128)S(1)}, u32[]{:S(2)}, u32[]{:S(2)}) collective-permute-start(f32[8,208]{1,0:T(8,128)S(1)} %multiply_select_fusion.c_ref), channel_id=1, source_target_pairs={{0,14},{2,0},{4,2},{6,4},{8,6},{10,8},{12,10},{14,12},{1,15},{3,1}... | collective-permute-start | bytes 19976 | tf_op jit(solution)/shard_map/ppermute | solution.py:27
  16.5 19.4 %collective-permute-start.6 = (f32[8,208]{1,0:T(8,128)S(1)}, f32[8,208]{1,0:T(8,128)S(1)}, u32[]{:S(2)}, u32[]{:S(2)}) collective-permute-start(f32[8,208]{1,0:T(8,128)S(1)} %multiply_select_fusion.c_ref), channel_id=1, source_target_pairs={{0,2},{2,4},{4,6},{6,8},{8,10},{10,12},{12,14},{14,0},{1,3},{3,5},... | collective-permute-start | bytes 19976 | tf_op jit(solution)/shard_map/ppermute | solution.py:27
  32.4 23.4 %collective-permute-start.11 = (bf16[208,1280]{1,0:T(8,128)(2,1)S(1)}, bf16[208,1280]{1,0:T(8,128)(2,1)S(1)}, u32[]{:S(2)}, u32[]{:S(2)}) collective-permute-start(bf16[208,1280]{1,0:T(8,128)(2,1)S(1)} %get-tuple-element.29), channel_id=1, source_target_pairs={{0,4},{2,6},{4,8},{6,10},{8,12},{10,14},{1,5},{3,7},{5,9},{7,11},{... | collective-permute-start | bytes 1597448 | tf_op jit(solution)/shard_map/ppermute | solution.py:27
  35.9 12.6 %collective-permute-start.5 = (f32[8,208]{1,0:T(8,128)S(1)}, f32[8,208]{1,0:T(8,128)S(1)}, u32[]{:S(2)}, u32[]{:S(2)}) collective-permute-start(f32[8,208]{1,0:T(8,128)S(1)} %multiply_select_fusion.c_ref), channel_id=1, source_target_pairs={{0,4},{2,6},{4,8},{6,10},{8,12},{10,14},{12,0},{14,2},{1,5},{3,7},... | collective-permute-start | bytes 19976 | tf_op jit(solution)/shard_map/ppermute | solution.py:27
  37.5 22.4 %collective-permute-start.12 = (bf16[208,1280]{1,0:T(8,128)(2,1)S(1)}, bf16[208,1280]{1,0:T(8,128)(2,1)S(1)}, u32[]{:S(2)}, u32[]{:S(2)}) collective-permute-start(bf16[208,1280]{1,0:T(8,128)(2,1)S(1)} %collective-permute-done.10.near_ref), channel_id=1, source_target_pairs={{0,4},{4,8},{6,2},{8,12},{10,6},{14,10},{1,5},{5,9},{7,3},{9,13},{... | collective-permute-start | bytes 1597448 | tf_op jit(solution)/shard_map/ppermute | solution.py:27
  40.1 14.4 %copy-start.3 = (s32[8]{0:T(128)S(1)}, s32[8]{0:T(128)}, u32[]{:S(2)}) copy-start(s32[8]{0:T(128)} %pos_ref.1) | copy-start | bytes 100
  40.1 19.8 %copy-start.1 = (f32[1,3,2560]{2,0,1:T(1,128)S(1)}, f32[1,3,2560]{2,0,1:T(1,128)}, u32[]{:S(2)}) copy-start(f32[1,3,2560]{2,0,1:T(1,128)} %param.13) | copy-start | bytes 92164
  40.1 19.8 %copy-start.2 = (f32[1,3,2560]{2,0,1:T(1,128)S(1)}, f32[1,3,2560]{2,0,1:T(1,128)}, u32[]{:S(2)}) copy-start(f32[1,3,2560]{2,0,1:T(1,128)} %param.14) | copy-start | bytes 92164
  48.5 20.8 %collective-permute-start.8 = (bf16[208,1280]{1,0:T(8,128)(2,1)S(1)}, bf16[208,1280]{1,0:T(8,128)(2,1)S(1)}, u32[]{:S(2)}, u32[]{:S(2)}) collective-permute-start(bf16[208,1280]{1,0:T(8,128)(2,1)S(1)} %get-tuple-element.18), channel_id=1, source_target_pairs={{0,4},{4,8},{8,12},{1,5},{5,9},{9,13},{16,20},{20,24},{24,28},{17,... | collective-permute-start | bytes 1597448 | tf_op jit(solution)/shard_map/ppermute | solution.py:27
  53.0 16.4 %collective-permute-start.9 = (bf16[208,1280]{1,0:T(8,128)(2,1)S(1)}, bf16[208,1280]{1,0:T(8,128)(2,1)S(1)}, u32[]{:S(2)}, u32[]{:S(2)}) collective-permute-start(bf16[208,1280]{1,0:T(8,128)(2,1)S(1)} %collective-permute-done.1.ahead_ref), channel_id=1, source_target_pairs={{0,2},{2,0},{4,6},{6,4},{8,10},{10,8},{12,14},{14,12},{1,3},{3,1},... | collective-permute-start | bytes 1597448 | tf_op jit(solution)/shard_map/ppermute | solution.py:27
  53.1 16.3 %collective-permute-start.2 = (bf16[208,1280]{1,0:T(8,128)(2,1)S(1)}, bf16[208,1280]{1,0:T(8,128)(2,1)S(1)}, u32[]{:S(2)}, u32[]{:S(2)}) collective-permute-start(bf16[208,1280]{1,0:T(8,128)(2,1)S(1)} %collective-permute-done.near_ref), channel_id=1, source_target_pairs={{6,2},{10,6},{14,10},{7,3},{11,7},{15,11},{22,18},{26,22},{30,26},... | collective-permute-start | bytes 1597448 | tf_op jit(solution)/shard_map/ppermute | solution.py:27

commit v2 on v1

--- a/solution.py
+++ b/solution.py
@@ -12,6 +12,7 @@
 HW_DEV = 104
 PERIOD = 256
 CHUNKS = 2
+FIRST = 0.5
 SUM_HEADS = 5
 LIMIT = 24 << 20
 F32 = jnp.float32
@@ -287,7 +288,7 @@
     near_ref, own_ref, ahead_ref, across_ref, base_ref, amp_ref, q_ref, k_ref, v_ref,
     mean_ref, rstd_ref, ck_ref, sk_ref, cq_ref, sq_ref, emb_ref, step_ref, *rest,
 ):
-    vel_hbm, new_hbm, keys, wide, queries, vel_out, new_out, sems = rest[-8:]
+    vel_hbm, new_hbm, keys, values, counted, queries, vel_out, new_out, sems = rest[-9:]
     count = own_ref.shape[0]
     two = 2 * size
     first = lo // 2
@@ -342,10 +343,10 @@
             value = raw[:, half[i]]
             part = key[i]
             if g in there:
-                part = jnp.where(there[g], part, keys[slot, rows(2), half[i]])
+                part = jnp.where(there[g], part, keys[slot, i, rows(2)])
                 value = jnp.where(there[g], value, jnp.zeros_like(value))
-            keys[slot, rows(g), half[i]] = part
-            wide[slot, i, rows(g), :size] = value
+            keys[slot, i, rows(g)] = part
+            values[slot, i, rows(g)] = value
         if g in (1, 2):
             raw = jnp.dot(mixed, q_ref[first + pair], preferred_element_type=F32)
             parts = turned(raw, cq_ref[g - 1], sq_ref[g - 1])
@@ -353,23 +354,31 @@
             for side in range(2):
                 mine = (lane < size // 2) == (side == 0)
                 for i in range(2):
-                    queries[slot, g - 1, rows(side), half[i]] = jnp.where(mine, parts[i], jnp.zeros_like(parts[i]))
-
-    def score(slot, g):
+                    queries[slot, i, rows(2 * (g - 1) + side)] = jnp.where(mine, parts[i], jnp.zeros_like(parts[i]))
+
+    def dot_keys(slot, query_rows, span):
         return lax.dot_general(
-            queries[slot, g],
-            keys[slot, g * count : (g + 3) * count],
+            jnp.concatenate([queries[slot, i, query_rows] for i in range(2)], axis=1),
+            jnp.concatenate([keys[slot, i, span] for i in range(2)], axis=1),
             (((1,), (1,)), ((), ())),
             preferred_element_type=F32,
         )
 
-    def soften(scores):
-        top = jnp.max(scores, axis=-1, keepdims=True)
-        return jnp.exp2(scores - top).astype(BF16)
-
-    def gather(slot, side, g, weights):
-        total = jnp.dot(weights, wide[slot, side, g * count : (g + 3) * count], preferred_element_type=F32)
-        return total[:, :size] / total[:, size:]
+    def soften(shared, single):
+        top = jnp.maximum(jnp.max(shared, axis=-1, keepdims=True), jnp.max(single, axis=-1, keepdims=True))
+        return jnp.exp2(shared - top).astype(BF16), jnp.exp2(single - top).astype(BF16)
+
+    def gather(slot, side, weights):
+        wide = lambda span: jnp.concatenate([values[slot, side, span], counted[span]], axis=1)
+        common = slice(count, 3 * count)
+        total = jnp.dot(
+            jnp.concatenate([shared for shared, _ in weights], axis=0), wide(common), preferred_element_type=F32
+        )
+        outs = []
+        for g, own in ((0, 0), (1, 3)):
+            part = total[rows(g)] + jnp.dot(weights[g][1], wide(rows(own)), preferred_element_type=F32)
+            outs.append(part[:, :size] / part[:, size:])
+        return outs
 
     def finish(pair, slot, side, g, attn):
         x = tokens(pair, side, g + 1)
@@ -399,20 +408,20 @@
                 for copy in copies(pair - 2, slot):
                     copy.wait()
 
-        for g, groups in ((0, (2, 1)), (1, (0, 3))):
-            scores = score(slot, g)
+        shared = dot_keys(slot, slice(0, 4 * count), slice(count, 3 * count))
+        single = [
+            dot_keys(slot, slice(0, 2 * count), rows(0)),
+            dot_keys(slot, slice(2 * count, 4 * count), rows(3)),
+        ]
+        for side, groups in ((0, (2, 1)), (1, (0, 3))):
             if following:
                 mixed = [mix(pair + 1, j) for j in groups]
-            weights = soften(scores[rows(0)])
+            weights = [soften(shared[rows(2 * g + side)], single[g][rows(side)]) for g in range(2)]
             if following:
-                project(pair + 1, other, groups[0], mixed[0])
-            total = gather(slot, 0, g, weights)
-            weights = soften(scores[rows(1)])
-            finish(pair, slot, 0, g, total)
-            if following:
-                project(pair + 1, other, groups[1], mixed[1])
-            total = gather(slot, 1, g, weights)
-            finish(pair, slot, 1, g, total)
+                for j, m in zip(groups, mixed):
+                    project(pair + 1, other, j, m)
+            for g, total in enumerate(gather(slot, side, weights)):
+                finish(pair, slot, side, g, total)
         for copy in copies(pair, slot):
             copy.start()
 
@@ -421,9 +430,7 @@
         ones = jnp.ones((count, size), BF16)
         if g in there:
             ones = jnp.where(there[g], ones, jnp.zeros_like(ones))
-        for slot in range(2):
-            for side in range(2):
-                wide[slot, side, rows(g), size:] = ones
+        counted[rows(g)] = ones
     for g in (2, 1, 0, 3):
         project(0, 0, g, mix(0, g))
     looped = (pairs - 1) // 2
@@ -454,9 +461,10 @@
         out_specs=[hbm] * 2,
         out_shape=[jax.ShapeDtypeStruct(own.shape, BF16)] * 2,
         scratch_shapes=[
-            pltpu.VMEM((2, 4 * count, 2 * size), BF16),
-            pltpu.VMEM((2, 2, 4 * count, 2 * size), BF16),
-            pltpu.VMEM((2, 2, 2 * count, 2 * size), BF16),
+            pltpu.VMEM((2, 2, 4 * count, size), BF16),
+            pltpu.VMEM((2, 2, 4 * count, size), BF16),
+            pltpu.VMEM((4 * count, size), BF16),
+            pltpu.VMEM((2, 2, 4 * count, size), BF16),
             pltpu.VMEM((2, count, 2 * size), BF16),
             pltpu.VMEM((2, count, 2 * size), BF16),
             pltpu.SemaphoreType.DMA((2, 2)),
@@ -480,7 +488,7 @@
     base = mod_base[0][:, None, :]
     amp = mod_amp[0][:, None, :]
 
-    cuts = [2 * (local_heads // 2 * i // CHUNKS) for i in range(CHUNKS)] + [local_heads]
+    cuts = [0, 2 * max(1, int(local_heads // 2 * FIRST)), local_heads]
     *pieces, rows, sums = split(hidden, cuts, size)
     swap = [(i, i ^ 1) for i in everyone]
     two_on = [(i, i + 2) for i in everyone]

time: 78.8 us -> 78.3 us (level)
  Pallas kernels: 23.6 us -> 22.5 us
    pallas_call x2, Pallas kernels: 18.1 us -> 16.9 us  [attend(): pl.pallas_call(functools.partial(attend_kernel, lo, number, size, bool(re...]
  transfers between devices with their start and end apart: 13 -> 13, of which waited for: 6 -> 6; matrix products, arithmetic and copies ran while one was open for 2% -> 3% of each run, Pallas kernels for 16% -> 16%
where the time goes in v2:
time: 78.3 us; the launch traced here: 78 us
  waiting for transfers between devices  29.9 us (38%)
  Pallas kernels  22.5 us (29%)
  starting transfers between devices  21.9 us (28%)
  matrix products  1.72 us (2%)
  between operations  1.71 us (2%)
    ppermute x11, waiting for transfers between devices, send(): return lax.ppermute(array, 'queue', pairs)  28.8 us
    ppermute x11, starting transfers between devices, send(): return lax.ppermute(array, 'queue', pairs)  21.7 us
    pallas_call x2, Pallas kernels, attend(): pl.pallas_call(functools.partial(attend_kernel, lo, number, size, bool(re...  16.9 us
    pallas_call x1, Pallas kernels, token_squares(): pl.pallas_call(functools.partial(squares_kernel, width), name='token_squa...  2.61 us
    dot_general x3, matrix products, block_maps(): jnp.einsum('pde,ef->pdf', weight.reshape(heads // 2, 2 * size, size), spr...  1.72 us
    pallas_call x1, Pallas kernels, split(): pl.pallas_call(functools.partial(split_kernel, size, cuts), name='token_s...  1.66 us
  transfers between devices with their start and end apart: 13, of which 6 were waited for; matrix products, arithmetic and copies ran while one was open for 3% of the time, Pallas kernels for 16%

profile of v2, /device:TPU:0, one launch (start us, length us, event | category | flops | bytes accessed | tf_op | source)
XLA Modules:
  0.0 78.0 jit_solution(9927775454028294375)
XLA Ops:
  0.6 0.0 copy-start
  0.6 1.7 %token_split.1 = (bf16[208,1280]{1,0:T(8,128)(2,1)S(1)}, bf16[208,1280]{1,0:T(8,128)(2,1)S(1)}, bf16[208,2560]{1,0:T(8,128)(2,1)S(1)}, f32[8,208]{1,0:T(8,128)S(1)}) custom-call(bf16[208,2560]{1,0:T(8,128)(2,1)} %x_hbm.1), custom_call_target="tpu_custom_call" | custom-call | flops 2129920 | bytes 2129920 | tf_op jit(solution)/shard_map/token_split/pallas_call | solution.py:130
  2.3 0.7 collective-permute-start.1
  3.0 5.9 %collective-permute-start = (bf16[208,1280]{1,0:T(8,128)(2,1)S(1)}, bf16[208,1280]{1,0:T(8,128)(2,1)S(1)}, u32[]{:S(2)}, u32[]{:S(2)}) collective-permute-start(bf16[208,1280]{1,0:T(8,128)(2,1)S(1)} %get-tuple-element.18), channel_id=1, source_target_pairs={{0,2},{2,0},{4,6},{6,4},{8,10},{10,8},{12,14},{14,12},{1,3},{3,1},... | collective-permute-start | bytes 1597448 | tf_op jit(solution)/shard_map/ppermute | solution.py:28
  8.9 0.0 collective-permute-start.3
  8.9 0.2 collective-permute-start.10
  9.0 0.0 copy-start.4
  9.0 0.1 broadcast_compare_fusion
  9.9 0.1 collective-permute-done.3.peer_ref
  10.0 2.6 %token_squares.1 = f32[8,208]{1,0:T(8,128)S(1)} custom-call(s32[1]{0:T(128)S(6)} %copy.21.level_ref, s32[65]{0:T(128)} %steps_hbm.1, bf16[208,2560]{1,0:T(8,128)(2,1)S(1)} %get-tuple-element.19.x_ref.own_ref, f32[8,208]{1,0:T(8,128)S(1)} %get-tuple-element.20.own_ref, f32[8,208]{1,0:T(8,128)S(1)} %collective-permute-done.3.peer_ref, f32[3,1,2560]{2,1,0:T(1,128)} %bitcast.28, ...), custom_call_target="tpu_custom_call" | custom-call | flops 272629760 | bytes 2375680 | tf_op jit(solution)/shard_map/token_squares/pallas_call | solution.py:204
  12.7 0.0 copy-start.5
  12.7 0.3 collective-permute-start.4
  13.0 0.9 %collective-permute-done.4 = f32[8,208]{1,0:T(8,128)S(1)} collective-permute-done((f32[8,208]{1,0:T(8,128)S(1)}, f32[8,208]{1,0:T(8,128)S(1)}, u32[]{:S(2)}, u32[]{:S(2)}) %collective-permute-start.4) | collective-permute-done | bytes 6688 | tf_op jit(solution)/shard_map/ppermute | solution.py:33
  13.9 0.1 multiply_select_fusion.c_ref
  14.0 2.6 %collective-permute-start.7 = (f32[8,208]{1,0:T(8,128)S(1)}, f32[8,208]{1,0:T(8,128)S(1)}, u32[]{:S(2)}, u32[]{:S(2)}) collective-permute-start(f32[8,208]{1,0:T(8,128)S(1)} %multiply_select_fusion.c_ref), channel_id=1, source_target_pairs={{0,14},{2,0},{4,2},{6,4},{8,6},{10,8},{12,10},{14,12},{1,15},{3,1}... | collective-permute-start | bytes 19976 | tf_op jit(solution)/shard_map/ppermute | solution.py:28
  16.5 0.0 collective-permute-start.6
  16.5 0.0 copy-done.4
  16.5 0.6 fusion.1.k_ref
  17.1 15.3 %collective-permute-done.7.d_ref = f32[8,208]{1,0:T(8,128)S(1)} collective-permute-done((f32[8,208]{1,0:T(8,128)S(1)}, f32[8,208]{1,0:T(8,128)S(1)}, u32[]{:S(2)}, u32[]{:S(2)}) %collective-permute-start.7) | collective-permute-done | bytes 6688 | tf_op jit(solution)/shard_map/ppermute | solution.py:28
  32.4 3.5 %collective-permute-start.11 = (bf16[208,1280]{1,0:T(8,128)(2,1)S(1)}, bf16[208,1280]{1,0:T(8,128)(2,1)S(1)}, u32[]{:S(2)}, u32[]{:S(2)}) collective-permute-start(bf16[208,1280]{1,0:T(8,128)(2,1)S(1)} %get-tuple-element.29), channel_id=1, source_target_pairs={{0,4},{2,6},{4,8},{6,10},{8,12},{10,14},{1,5},{3,7},{5,9},{7,11},{... | collective-permute-start | bytes 1597448 | tf_op jit(solution)/shard_map/ppermute | solution.py:28
  35.9 0.0 collective-permute-done.6.b_ref
  35.9 1.6 %collective-permute-start.5 = (f32[8,208]{1,0:T(8,128)S(1)}, f32[8,208]{1,0:T(8,128)S(1)}, u32[]{:S(2)}, u32[]{:S(2)}) collective-permute-start(f32[8,208]{1,0:T(8,128)S(1)} %multiply_select_fusion.c_ref), channel_id=1, source_target_pairs={{0,4},{2,6},{4,8},{6,10},{8,12},{10,14},{12,0},{14,2},{1,5},{3,7},... | collective-permute-start | bytes 19976 | tf_op jit(solution)/shard_map/ppermute | solution.py:28
  37.5 0.0 collective-permute-done.10.near_ref
  37.5 2.0 %collective-permute-start.12 = (bf16[208,1280]{1,0:T(8,128)(2,1)S(1)}, bf16[208,1280]{1,0:T(8,128)(2,1)S(1)}, u32[]{:S(2)}, u32[]{:S(2)}) collective-permute-start(bf16[208,1280]{1,0:T(8,128)(2,1)S(1)} %collective-permute-done.10.near_ref), channel_id=1, source_target_pairs={{0,4},{4,8},{6,2},{8,12},{10,6},{14,10},{1,5},{5,9},{7,3},{9,13},{... | collective-permute-start | bytes 1597448 | tf_op jit(solution)/shard_map/ppermute | solution.py:28
  39.5 0.0 copy-done.5
  39.5 0.6 fusion.2.q_ref
  40.1 0.0 copy-start.3
  40.1 0.0 copy-start.1
  40.1 0.0 copy-start.2
  40.1 8.4 %collective-permute-done.5.a_ref = f32[8,208]{1,0:T(8,128)S(1)} collective-permute-done((f32[8,208]{1,0:T(8,128)S(1)}, f32[8,208]{1,0:T(8,128)S(1)}, u32[]{:S(2)}, u32[]{:S(2)}) %collective-permute-start.5) | collective-permute-done | bytes 6688 | tf_op jit(solution)/shard_map/ppermute | solution.py:28
  48.5 4.4 %collective-permute-start.8 = (bf16[208,1280]{1,0:T(8,128)(2,1)S(1)}, bf16[208,1280]{1,0:T(8,128)(2,1)S(1)}, u32[]{:S(2)}, u32[]{:S(2)}) collective-permute-start(bf16[208,1280]{1,0:T(8,128)(2,1)S(1)} %get-tuple-element.18), channel_id=1, source_target_pairs={{0,4},{4,8},{8,12},{1,5},{5,9},{9,13},{16,20},{20,24},{24,28},{17,... | collective-permute-start | bytes 1597448 | tf_op jit(solution)/shard_map/ppermute | solution.py:28
  53.0 0.0 collective-permute-done.1.ahead_ref
  53.0 0.1 collective-permute-start.9
  53.0 0.0 collective-permute-done.near_ref
  53.1 0.9 %collective-permute-start.2 = (bf16[208,1280]{1,0:T(8,128)(2,1)S(1)}, bf16[208,1280]{1,0:T(8,128)(2,1)S(1)}, u32[]{:S(2)}, u32[]{:S(2)}) collective-permute-start(bf16[208,1280]{1,0:T(8,128)(2,1)S(1)} %collective-permute-done.near_ref), channel_id=1, source_target_pairs={{6,2},{10,6},{14,10},{7,3},{11,7},{15,11},{22,18},{26,22},{30,26},... | collective-permute-start | bytes 1597448 | tf_op jit(solution)/shard_map/ppermute | solution.py:28
  53.9 0.0 copy-done
  54.0 0.6 fusion.v_ref
  54.5 0.0 copy-done.3
  54.6 1.3 %token_tables.1 = (f32[4,208,128]{2,1,0:T(8,128)S(1)}, f32[4,208,128]{2,1,0:T(8,128)S(1)}, f32[4,208,128]{2,1,0:T(8,128)S(1)}, f32[4,208,128]{2,1,0:T(8,128)S(1)...) custom-call(s32[8]{0:T(128)S(1)} %copy-done.3, ...), custom_call_target="tpu_custom_call" | custom-call | flops 1597440 | bytes 2129920 | tf_op jit(solution)/shard_map/token_tables/pallas_call | solution.py:274
  55.8 0.0 collective-permute-done.11.ahead_ref
  55.8 4.1 %collective-permute-done.12.across_ref = bf16[208,1280]{1,0:T(8,128)(2,1)S(1)} collective-permute-done((bf16[208,1280]{1,0:T(8,128)(2,1)S(1)}, bf16[208,1280]{1,0:T(8,128)(2,1)S(1)}, u32[]{:S(2)}, u32[]{:S(2)}) %collective-permute-start.12) | collective-permute-done | bytes 532512 | tf_op jit(solution)/shard_map/ppermute | solution.py:28
  60.0 0.0 copy-done.1
  60.0 0.0 copy-done.2
  60.0 8.5 %attend_heads.2 = (bf16[208,2560]{1,0:T(8,128)(2,1)}, bf16[208,2560]{1,0:T(8,128)(2,1)}) custom-call(bf16[208,1280]{1,0:T(8,128)(2,1)S(1)} %collective-permute-done.10.near_ref, bf16[208,2560]{1,0:T(8,128)(2,1)S(1)} %get-tuple-element.19.x_ref.own_ref, bf16[208,1280]{1,0:T(8,128)(2,1)S(1)} %collective-permute-done.11.ahead_ref, ...), custom_call_target="tpu_custom_call" | custom-call | flops 2010644480 | bytes 4833280 | tf_op jit(solution)/shard_map/attend_heads/pallas_call | solution.py:457
  68.4 1.0 %collective-permute-done.8.rest_0_ = bf16[208,1280]{1,0:T(8,128)(2,1)S(1)} collective-permute-done((bf16[208,1280]{1,0:T(8,128)(2,1)S(1)}, bf16[208,1280]{1,0:T(8,128)(2,1)S(1)}, u32[]{:S(2)}, u32[]{:S(2)}) %collective-permute-start.8) | collective-permute-done | bytes 532512 | tf_op jit(solution)/shard_map/ppermute | solution.py:28
  69.4 0.0 collective-permute-done.9.rest_1_
  69.4 0.0 collective-permute-done.2.across_ref
  69.4 8.5 %attend_heads.3 = (bf16[208,2560]{1,0:T(8,128)(2,1)}, bf16[208,2560]{1,0:T(8,128)(2,1)}) custom-call(bf16[208,1280]{1,0:T(8,128)(2,1)S(1)} %collective-permute-done.near_ref, bf16[208,2560]{1,0:T(8,128)(2,1)S(1)} %get-tuple-element.19.x_ref.own_ref, ...), custom_call_target="tpu_custom_call", output_to_operand_aliasing={{0}: (19, {}), {1}: (20, {})} | custom-call | flops 2010644480 | bytes 4833280 | tf_op jit(solution)/shard_map/attend_heads/pallas_call | solution.py:457
  (5 shorter events, 0.0 us)
Async XLA Ops:
  0.6 53.3 %copy-start = (bf16[1,20,128,128]{3,2,1,0:T(8,128)(2,1)S(1)}, bf16[1,20,128,128]{3,2,1,0:T(8,128)(2,1)}, u32[]{:S(2)}) copy-start(bf16[1,20,128,128]{3,2,1,0:T(8,128)(2,1)} %param.12) | copy-start | bytes 1966084
  2.3 50.6 %collective-permute-start.1 = (bf16[208,1280]{1,0:T(8,128)(2,1)S(1)}, bf16[208,1280]{1,0:T(8,128)(2,1)S(1)}, u32[]{:S(2)}, u32[]{:S(2)}) collective-permute-start(bf16[208,1280]{1,0:T(8,128)(2,1)S(1)} %get-tuple-element.18), channel_id=1, source_target_pairs={{2,6},{6,10},{10,14},{3,7},{7,11},{11,15},{18,22},{22,26},{26,30},... | collective-permute-start | bytes 1597448 | tf_op jit(solution)/shard_map/ppermute | solution.py:28
  3.0 50.0 %collective-permute-start = (bf16[208,1280]{1,0:T(8,128)(2,1)S(1)}, bf16[208,1280]{1,0:T(8,128)(2,1)S(1)}, u32[]{:S(2)}, u32[]{:S(2)}) collective-permute-start(bf16[208,1280]{1,0:T(8,128)(2,1)S(1)} %get-tuple-element.18), channel_id=1, source_target_pairs={{0,2},{2,0},{4,6},{6,4},{8,10},{10,8},{12,14},{14,12},{1,3},{3,1},... | collective-permute-start | bytes 1597448 | tf_op jit(solution)/shard_map/ppermute | solution.py:28
  8.9 1.2 %collective-permute-start.3 = (f32[8,208]{1,0:T(8,128)S(1)}, f32[8,208]{1,0:T(8,128)S(1)}, u32[]{:S(2)}, u32[]{:S(2)}) collective-permute-start(f32[8,208]{1,0:T(8,128)S(1)} %get-tuple-element.20.own_ref), channel_id=1, source_target_pairs={{0,1},{1,0},{2,3},{3,2},{4,5},{5,4},{6,7},{7,6},{8,9},{9,8},{10,11... | collective-permute-start | bytes 19976 | tf_op jit(solution)/shard_map/ppermute | solution.py:33
  8.9 28.7 %collective-permute-start.10 = (bf16[208,1280]{1,0:T(8,128)(2,1)S(1)}, bf16[208,1280]{1,0:T(8,128)(2,1)S(1)}, u32[]{:S(2)}, u32[]{:S(2)}) collective-permute-start(bf16[208,1280]{1,0:T(8,128)(2,1)S(1)} %get-tuple-element.29), channel_id=1, source_target_pairs={{0,2},{2,0},{4,6},{6,4},{8,10},{10,8},{12,14},{14,12},{1,3},{3,1},... | collective-permute-start | bytes 1597448 | tf_op jit(solution)/shard_map/ppermute | solution.py:28
  9.0 7.5 %copy-start.4 = (bf16[1,20,128,128]{3,2,1,0:T(8,128)(2,1)S(1)}, bf16[1,20,128,128]{3,2,1,0:T(8,128)(2,1)}, u32[]{:S(2)}) copy-start(bf16[1,20,128,128]{3,2,1,0:T(8,128)(2,1)} %k_hbm.1) | copy-start | bytes 1966084
  12.7 26.9 %copy-start.5 = (bf16[1,20,128,128]{3,2,1,0:T(8,128)(2,1)S(1)}, bf16[1,20,128,128]{3,2,1,0:T(8,128)(2,1)}, u32[]{:S(2)}) copy-start(bf16[1,20,128,128]{3,2,1,0:T(8,128)(2,1)} %q_hbm.1) | copy-start | bytes 1966084
  12.7 1.2 %collective-permute-start.4 = (f32[8,208]{1,0:T(8,128)S(1)}, f32[8,208]{1,0:T(8,128)S(1)}, u32[]{:S(2)}, u32[]{:S(2)}) collective-permute-start(f32[8,208]{1,0:T(8,128)S(1)} %token_squares.1), channel_id=1, source_target_pairs={{0,1},{1,0},{2,3},{3,2},{4,5},{5,4},{6,7},{7,6},{8,9},{9,8},{10,11... | collective-permute-start | bytes 19976 | tf_op jit(solution)/shard_map/ppermute | solution.py:33
  14.0 18.5 %collective-permute-start.7 = (f32[8,208]{1,0:T(8,128)S(1)}, f32[8,208]{1,0:T(8,128)S(1)}, u32[]{:S(2)}, u32[]{:S(2)}) collective-permute-start(f32[8,208]{1,0:T(8,128)S(1)} %multiply_select_fusion.c_ref), channel_id=1, source_target_pairs={{0,14},{2,0},{4,2},{6,4},{8,6},{10,8},{12,10},{14,12},{1,15},{3,1}... | collective-permute-start | bytes 19976 | tf_op jit(solution)/shard_map/ppermute | solution.py:28
  16.5 19.4 %collective-permute-start.6 = (f32[8,208]{1,0:T(8,128)S(1)}, f32[8,208]{1,0:T(8,128)S(1)}, u32[]{:S(2)}, u32[]{:S(2)}) collective-permute-start(f32[8,208]{1,0:T(8,128)S(1)} %multiply_select_fusion.c_ref), channel_id=1, source_target_pairs={{0,2},{2,4},{4,6},{6,8},{8,10},{10,12},{12,14},{14,0},{1,3},{3,5},... | collective-permute-start | bytes 19976 | tf_op jit(solution)/shard_map/ppermute | solution.py:28
  32.4 23.4 %collective-permute-start.11 = (bf16[208,1280]{1,0:T(8,128)(2,1)S(1)}, bf16[208,1280]{1,0:T(8,128)(2,1)S(1)}, u32[]{:S(2)}, u32[]{:S(2)}) collective-permute-start(bf16[208,1280]{1,0:T(8,128)(2,1)S(1)} %get-tuple-element.29), channel_id=1, source_target_pairs={{0,4},{2,6},{4,8},{6,10},{8,12},{10,14},{1,5},{3,7},{5,9},{7,11},{... | collective-permute-start | bytes 1597448 | tf_op jit(solution)/shard_map/ppermute | solution.py:28
  35.9 12.6 %collective-permute-start.5 = (f32[8,208]{1,0:T(8,128)S(1)}, f32[8,208]{1,0:T(8,128)S(1)}, u32[]{:S(2)}, u32[]{:S(2)}) collective-permute-start(f32[8,208]{1,0:T(8,128)S(1)} %multiply_select_fusion.c_ref), channel_id=1, source_target_pairs={{0,4},{2,6},{4,8},{6,10},{8,12},{10,14},{12,0},{14,2},{1,5},{3,7},... | collective-permute-start | bytes 19976 | tf_op jit(solution)/shard_map/ppermute | solution.py:28
  37.5 22.4 %collective-permute-start.12 = (bf16[208,1280]{1,0:T(8,128)(2,1)S(1)}, bf16[208,1280]{1,0:T(8,128)(2,1)S(1)}, u32[]{:S(2)}, u32[]{:S(2)}) collective-permute-start(bf16[208,1280]{1,0:T(8,128)(2,1)S(1)} %collective-permute-done.10.near_ref), channel_id=1, source_target_pairs={{0,4},{4,8},{6,2},{8,12},{10,6},{14,10},{1,5},{5,9},{7,3},{9,13},{... | collective-permute-start | bytes 1597448 | tf_op jit(solution)/shard_map/ppermute | solution.py:28
  40.1 14.4 %copy-start.3 = (s32[8]{0:T(128)S(1)}, s32[8]{0:T(128)}, u32[]{:S(2)}) copy-start(s32[8]{0:T(128)} %pos_ref.1) | copy-start | bytes 100
  40.1 19.8 %copy-start.1 = (f32[1,3,2560]{2,0,1:T(1,128)S(1)}, f32[1,3,2560]{2,0,1:T(1,128)}, u32[]{:S(2)}) copy-start(f32[1,3,2560]{2,0,1:T(1,128)} %param.13) | copy-start | bytes 92164
  40.1 19.8 %copy-start.2 = (f32[1,3,2560]{2,0,1:T(1,128)S(1)}, f32[1,3,2560]{2,0,1:T(1,128)}, u32[]{:S(2)}) copy-start(f32[1,3,2560]{2,0,1:T(1,128)} %param.14) | copy-start | bytes 92164
  48.5 20.8 %collective-permute-start.8 = (bf16[208,1280]{1,0:T(8,128)(2,1)S(1)}, bf16[208,1280]{1,0:T(8,128)(2,1)S(1)}, u32[]{:S(2)}, u32[]{:S(2)}) collective-permute-start(bf16[208,1280]{1,0:T(8,128)(2,1)S(1)} %get-tuple-element.18), channel_id=1, source_target_pairs={{0,4},{4,8},{8,12},{1,5},{5,9},{9,13},{16,20},{20,24},{24,28},{17,... | collective-permute-start | bytes 1597448 | tf_op jit(solution)/shard_map/ppermute | solution.py:28
  53.0 16.4 %collective-permute-start.9 = (bf16[208,1280]{1,0:T(8,128)(2,1)S(1)}, bf16[208,1280]{1,0:T(8,128)(2,1)S(1)}, u32[]{:S(2)}, u32[]{:S(2)}) collective-permute-start(bf16[208,1280]{1,0:T(8,128)(2,1)S(1)} %collective-permute-done.1.ahead_ref), channel_id=1, source_target_pairs={{0,2},{2,0},{4,6},{6,4},{8,10},{10,8},{12,14},{14,12},{1,3},{3,1},... | collective-permute-start | bytes 1597448 | tf_op jit(solution)/shard_map/ppermute | solution.py:28
  53.1 16.3 %collective-permute-start.2 = (bf16[208,1280]{1,0:T(8,128)(2,1)S(1)}, bf16[208,1280]{1,0:T(8,128)(2,1)S(1)}, u32[]{:S(2)}, u32[]{:S(2)}) collective-permute-start(bf16[208,1280]{1,0:T(8,128)(2,1)S(1)} %collective-permute-done.near_ref), channel_id=1, source_target_pairs={{6,2},{10,6},{14,10},{7,3},{11,7},{15,11},{22,18},{26,22},{30,26},... | collective-permute-start | bytes 1597448 | tf_op jit(solution)/shard_map/ppermute | solution.py:28

commit v3 on v2

--- a/solution.py
+++ b/solution.py
@@ -228,7 +228,7 @@
 
 
 def tables_kernel(
-    first, pos_ref, a_ref, b_ref, c_ref, d_ref,
+    first, pos_ref, a_ref, swap_ref, own_ref, other_ref,
     mean_ref, rstd_ref, ck_ref, sk_ref, cq_ref, sq_ref, emb_ref, step_ref,
 ):
     count, size = mean_ref.shape[1:]
@@ -245,11 +245,14 @@
     _, ffreq = pair_plan((8, size), size)
     emb_row = lax.broadcasted_iota(jnp.int32, emb_ref.shape, 0)
     moment = jnp.zeros(emb_ref.shape, F32)
-    for g, stats in enumerate((a_ref, b_ref, c_ref, d_ref)):
+    odd = position % 2 == 1
+    swapped, other = swap_ref[...], other_ref[...]
+    before, after = jnp.where(odd, swapped, other), jnp.where(odd, other, swapped)
+    for g, stats in enumerate((a_ref[...], before, own_ref[...], after)):
         start = pos_ref[jnp.clip(position + (g - 2), 0, last)]
         fangle = (start + row).astype(F32) * ffreq
         fcos, fsin = jnp.cos(fangle), jnp.sin(fangle)
-        cols = jnp.transpose(stats[...])
+        cols = jnp.transpose(stats)
         moment = jnp.where(emb_row == g, stats[4:5, 0:1], moment)
         for f in range(frames):
             lo, hi = f * HW_DEV, min((f + 1) * HW_DEV, count)
@@ -265,7 +268,7 @@
                 sq_ref[g - 1, lo:hi] = sin * column(2)
     channel = lax.broadcasted_iota(jnp.int32, emb_ref.shape, 1) + lax.axis_index("tp") * first
     emb_ref[...] = time_embed(moment, channel)
-    step_ref[...] = jnp.broadcast_to((b_ref[5:6, 0:size] - b_ref[4:5, 0:size]) / 1000.0, step_ref.shape)
+    step_ref[...] = jnp.broadcast_to((before[5:6, 0:size] - before[4:5, 0:size]) / 1000.0, step_ref.shape)
 
 
 def tables(stats, group_pos, first, count, size):
@@ -514,9 +517,9 @@
     own_stats = jnp.where((line == 2) | (line == 3), lax.rsqrt(total / width + 1e-06) * factor, squares)
     stats = [
         send(own_stats, [(i, i + 2) for i in everyone], length, wrap=True),
-        send(own_stats, [(i, i + 1) for i in everyone], length, wrap=True),
+        send(own_stats, swap, length),
         own_stats,
-        send(own_stats, [(i, i - 1) for i in everyone], length, wrap=True),
+        send(own_stats, [(i, i + 1 if i % 2 else i - 1) for i in everyone], length, wrap=length % 2 == 0),
     ]
     tabs = tables(stats, group_pos, local_width, count, size)
     q = block_maps(q_weight[0], True)

time: 78.3 us -> 68 us (0.87)
  waiting for transfers between devices: 29.9 us -> 19.5 us
    ppermute x11, waiting for transfers between devices: 28.8 us -> 18.4 us  [send(): return lax.ppermute(array, 'queue', pairs)]
  transfers between devices with their start and end apart: 13 -> 13, of which waited for: 6 -> 6; matrix products, arithmetic and copies ran while one was open for 3% -> 3% of each run, Pallas kernels for 16% -> 18%
where the time goes in v3:
time: 68 us; the launch traced here: 67.7 us
  Pallas kernels  22.5 us (33%)
  starting transfers between devices  22.1 us (32%)
  waiting for transfers between devices  19.5 us (29%)
  matrix products  1.73 us (3%)
  between operations  1.69 us (2%)
    ppermute x11, starting transfers between devices, send(): return lax.ppermute(array, 'queue', pairs)  21.8 us
    ppermute x11, waiting for transfers between devices, send(): return lax.ppermute(array, 'queue', pairs)  18.4 us
    pallas_call x2, Pallas kernels, attend(): pl.pallas_call(functools.partial(attend_kernel, lo, number, size, bool(re...  17 us
    pallas_call x1, Pallas kernels, token_squares(): pl.pallas_call(functools.partial(squares_kernel, width), name='token_squa...  2.61 us
    dot_general x3, matrix products, block_maps(): jnp.einsum('pde,ef->pdf', weight.reshape(heads // 2, 2 * size, size), spr...  1.73 us
    pallas_call x1, Pallas kernels, split(): pl.pallas_call(functools.partial(split_kernel, size, cuts), name='token_s...  1.66 us
  transfers between devices with their start and end apart: 13, of which 6 were waited for; matrix products, arithmetic and copies ran while one was open for 3% of the time, Pallas kernels for 18%

profile of v3, /device:TPU:0, one launch (start us, length us, event | category | flops | bytes accessed | tf_op | source)
XLA Modules:
  0.0 67.7 jit_solution(13698974880780074852)
XLA Ops:
  0.6 0.0 copy-start
  0.6 1.7 %token_split.1 = (bf16[208,1280]{1,0:T(8,128)(2,1)S(1)}, bf16[208,1280]{1,0:T(8,128)(2,1)S(1)}, bf16[208,2560]{1,0:T(8,128)(2,1)S(1)}, f32[8,208]{1,0:T(8,128)S(1)}) custom-call(bf16[208,2560]{1,0:T(8,128)(2,1)} %x_hbm.1), custom_call_target="tpu_custom_call" | custom-call | flops 2129920 | bytes 2129920 | tf_op jit(solution)/shard_map/token_split/pallas_call | solution.py:130
  2.3 0.7 %collective-permute-start.1 = (bf16[208,1280]{1,0:T(8,128)(2,1)S(1)}, bf16[208,1280]{1,0:T(8,128)(2,1)S(1)}, u32[]{:S(2)}, u32[]{:S(2)}) collective-permute-start(bf16[208,1280]{1,0:T(8,128)(2,1)S(1)} %get-tuple-element.18), channel_id=1, source_target_pairs={{2,6},{6,10},{10,14},{3,7},{7,11},{11,15},{18,22},{22,26},{26,30},... | collective-permute-start | bytes 1597448 | tf_op jit(solution)/shard_map/ppermute | solution.py:28
  3.0 5.9 %collective-permute-start = (bf16[208,1280]{1,0:T(8,128)(2,1)S(1)}, bf16[208,1280]{1,0:T(8,128)(2,1)S(1)}, u32[]{:S(2)}, u32[]{:S(2)}) collective-permute-start(bf16[208,1280]{1,0:T(8,128)(2,1)S(1)} %get-tuple-element.18), channel_id=1, source_target_pairs={{0,2},{2,0},{4,6},{6,4},{8,10},{10,8},{12,14},{14,12},{1,3},{3,1},... | collective-permute-start | bytes 1597448 | tf_op jit(solution)/shard_map/ppermute | solution.py:28
  8.9 0.0 collective-permute-start.3
  8.9 0.2 collective-permute-start.10
  9.0 0.0 copy-start.4
  9.0 0.1 broadcast_compare_fusion
  9.9 0.1 collective-permute-done.3.peer_ref
  10.0 2.6 %token_squares.1 = f32[8,208]{1,0:T(8,128)S(1)} custom-call(s32[1]{0:T(128)S(6)} %copy.21.level_ref, s32[65]{0:T(128)} %steps_hbm.1, bf16[208,2560]{1,0:T(8,128)(2,1)S(1)} %get-tuple-element.19.x_ref.own_ref, f32[8,208]{1,0:T(8,128)S(1)} %get-tuple-element.20.own_ref, f32[8,208]{1,0:T(8,128)S(1)} %collective-permute-done.3.peer_ref, f32[3,1,2560]{2,1,0:T(1,128)} %bitcast.28, ...), custom_call_target="tpu_custom_call" | custom-call | flops 272629760 | bytes 2375680 | tf_op jit(solution)/shard_map/token_squares/pallas_call | solution.py:204
  12.7 0.0 copy-start.5
  12.7 0.3 collective-permute-start.4
  13.0 0.9 %collective-permute-done.4 = f32[8,208]{1,0:T(8,128)S(1)} collective-permute-done((f32[8,208]{1,0:T(8,128)S(1)}, f32[8,208]{1,0:T(8,128)S(1)}, u32[]{:S(2)}, u32[]{:S(2)}) %collective-permute-start.4) | collective-permute-done | bytes 6688 | tf_op jit(solution)/shard_map/ppermute | solution.py:33
  13.9 0.1 multiply_select_fusion.own_ref
  14.0 2.6 %collective-permute-start.7 = (f32[8,208]{1,0:T(8,128)S(1)}, f32[8,208]{1,0:T(8,128)S(1)}, u32[]{:S(2)}, u32[]{:S(2)}) collective-permute-start(f32[8,208]{1,0:T(8,128)S(1)} %multiply_select_fusion.own_ref), channel_id=1, source_target_pairs={{0,14},{2,4},{4,2},{6,8},{8,6},{10,12},{12,10},{14,0},{1,15},{3,5}... | collective-permute-start | bytes 19976 | tf_op jit(solution)/shard_map/ppermute | solution.py:28
  16.5 0.5 collective-permute-start.6
  17.0 0.0 copy-done.4
  17.0 0.6 fusion.1.k_ref
  17.6 2.8 %collective-permute-done.7.other_ref = f32[8,208]{1,0:T(8,128)S(1)} collective-permute-done((f32[8,208]{1,0:T(8,128)S(1)}, f32[8,208]{1,0:T(8,128)S(1)}, u32[]{:S(2)}, u32[]{:S(2)}) %collective-permute-start.7) | collective-permute-done | bytes 6688 | tf_op jit(solution)/shard_map/ppermute | solution.py:28
  20.4 3.8 %collective-permute-start.11 = (bf16[208,1280]{1,0:T(8,128)(2,1)S(1)}, bf16[208,1280]{1,0:T(8,128)(2,1)S(1)}, u32[]{:S(2)}, u32[]{:S(2)}) collective-permute-start(bf16[208,1280]{1,0:T(8,128)(2,1)S(1)} %get-tuple-element.29), channel_id=1, source_target_pairs={{0,4},{2,6},{4,8},{6,10},{8,12},{10,14},{1,5},{3,7},{5,9},{7,11},{... | collective-permute-start | bytes 1597448 | tf_op jit(solution)/shard_map/ppermute | solution.py:28
  24.2 8.2 %collective-permute-done.6.swap_ref = f32[8,208]{1,0:T(8,128)S(1)} collective-permute-done((f32[8,208]{1,0:T(8,128)S(1)}, f32[8,208]{1,0:T(8,128)S(1)}, u32[]{:S(2)}, u32[]{:S(2)}) %collective-permute-start.6) | collective-permute-done | bytes 6688 | tf_op jit(solution)/shard_map/ppermute | solution.py:28
  32.4 1.5 %collective-permute-start.5 = (f32[8,208]{1,0:T(8,128)S(1)}, f32[8,208]{1,0:T(8,128)S(1)}, u32[]{:S(2)}, u32[]{:S(2)}) collective-permute-start(f32[8,208]{1,0:T(8,128)S(1)} %multiply_select_fusion.own_ref), channel_id=1, source_target_pairs={{0,4},{2,6},{4,8},{6,10},{8,12},{10,14},{12,0},{14,2},{1,5},{3,7},... | collective-permute-start | bytes 19976 | tf_op jit(solution)/shard_map/ppermute | solution.py:28
  34.0 0.0 collective-permute-done.10.near_ref
  34.0 3.5 %collective-permute-start.12 = (bf16[208,1280]{1,0:T(8,128)(2,1)S(1)}, bf16[208,1280]{1,0:T(8,128)(2,1)S(1)}, u32[]{:S(2)}, u32[]{:S(2)}) collective-permute-start(bf16[208,1280]{1,0:T(8,128)(2,1)S(1)} %collective-permute-done.10.near_ref), channel_id=1, source_target_pairs={{0,4},{4,8},{6,2},{8,12},{10,6},{14,10},{1,5},{5,9},{7,3},{9,13},{... | collective-permute-start | bytes 1597448 | tf_op jit(solution)/shard_map/ppermute | solution.py:28
  37.5 0.0 copy-done.5
  37.5 0.6 fusion.2.q_ref
  38.1 0.0 copy-start.3
  38.1 0.0 copy-start.1
  38.1 0.0 copy-start.2
  38.1 0.0 collective-permute-done.5.a_ref
  38.1 1.9 %collective-permute-start.8 = (bf16[208,1280]{1,0:T(8,128)(2,1)S(1)}, bf16[208,1280]{1,0:T(8,128)(2,1)S(1)}, u32[]{:S(2)}, u32[]{:S(2)}) collective-permute-start(bf16[208,1280]{1,0:T(8,128)(2,1)S(1)} %get-tuple-element.18), channel_id=1, source_target_pairs={{0,4},{4,8},{8,12},{1,5},{5,9},{9,13},{16,20},{20,24},{24,28},{17,... | collective-permute-start | bytes 1597448 | tf_op jit(solution)/shard_map/ppermute | solution.py:28
  40.1 0.0 collective-permute-done.1.ahead_ref
  40.1 0.4 collective-permute-start.9
  40.5 0.0 collective-permute-done.near_ref
  40.5 0.9 %collective-permute-start.2 = (bf16[208,1280]{1,0:T(8,128)(2,1)S(1)}, bf16[208,1280]{1,0:T(8,128)(2,1)S(1)}, u32[]{:S(2)}, u32[]{:S(2)}) collective-permute-start(bf16[208,1280]{1,0:T(8,128)(2,1)S(1)} %collective-permute-done.near_ref), channel_id=1, source_target_pairs={{6,2},{10,6},{14,10},{7,3},{11,7},{15,11},{22,18},{26,22},{30,26},... | collective-permute-start | bytes 1597448 | tf_op jit(solution)/shard_map/ppermute | solution.py:28
  41.4 0.0 copy-done
  41.4 0.6 fusion.v_ref
  42.0 0.0 copy-done.3
  42.0 1.3 %token_tables.1 = (f32[4,208,128]{2,1,0:T(8,128)S(1)}, f32[4,208,128]{2,1,0:T(8,128)S(1)}, f32[4,208,128]{2,1,0:T(8,128)S(1)}, f32[4,208,128]{2,1,0:T(8,128)S(1)...) custom-call(s32[8]{0:T(128)S(1)} %copy-done.3, ...), custom_call_target="tpu_custom_call" | custom-call | flops 1597440 | bytes 2129920 | tf_op jit(solution)/shard_map/token_tables/pallas_call | solution.py:277
  43.3 0.0 collective-permute-done.11.ahead_ref
  43.3 6.7 %collective-permute-done.12.across_ref = bf16[208,1280]{1,0:T(8,128)(2,1)S(1)} collective-permute-done((bf16[208,1280]{1,0:T(8,128)(2,1)S(1)}, bf16[208,1280]{1,0:T(8,128)(2,1)S(1)}, u32[]{:S(2)}, u32[]{:S(2)}) %collective-permute-start.12) | collective-permute-done | bytes 532512 | tf_op jit(solution)/shard_map/ppermute | solution.py:28
  49.9 0.0 copy-done.1
  49.9 0.0 copy-done.2
  50.0 8.5 %attend_heads.2 = (bf16[208,2560]{1,0:T(8,128)(2,1)}, bf16[208,2560]{1,0:T(8,128)(2,1)}) custom-call(bf16[208,1280]{1,0:T(8,128)(2,1)S(1)} %collective-permute-done.10.near_ref, bf16[208,2560]{1,0:T(8,128)(2,1)S(1)} %get-tuple-element.19.x_ref.own_ref, bf16[208,1280]{1,0:T(8,128)(2,1)S(1)} %collective-permute-done.11.ahead_ref, ...), custom_call_target="tpu_custom_call" | custom-call | flops 2010644480 | bytes 4833280 | tf_op jit(solution)/shard_map/attend_heads/pallas_call | solution.py:460
  58.4 0.7 collective-permute-done.8.rest_0_
  59.1 0.0 collective-permute-done.9.rest_1_
  59.1 0.0 collective-permute-done.2.across_ref
  59.1 8.5 %attend_heads.3 = (bf16[208,2560]{1,0:T(8,128)(2,1)}, bf16[208,2560]{1,0:T(8,128)(2,1)}) custom-call(bf16[208,1280]{1,0:T(8,128)(2,1)S(1)} %collective-permute-done.near_ref, bf16[208,2560]{1,0:T(8,128)(2,1)S(1)} %get-tuple-element.19.x_ref.own_ref, ...), custom_call_target="tpu_custom_call", output_to_operand_aliasing={{0}: (19, {}), {1}: (20, {})} | custom-call | flops 2010644480 | bytes 4833280 | tf_op jit(solution)/shard_map/attend_heads/pallas_call | solution.py:460
  (5 shorter events, 0.0 us)
Async XLA Ops:
  0.6 40.8 %copy-start = (bf16[1,20,128,128]{3,2,1,0:T(8,128)(2,1)S(1)}, bf16[1,20,128,128]{3,2,1,0:T(8,128)(2,1)}, u32[]{:S(2)}) copy-start(bf16[1,20,128,128]{3,2,1,0:T(8,128)(2,1)} %param.12) | copy-start | bytes 1966084
  2.3 37.8 %collective-permute-start.1 = (bf16[208,1280]{1,0:T(8,128)(2,1)S(1)}, bf16[208,1280]{1,0:T(8,128)(2,1)S(1)}, u32[]{:S(2)}, u32[]{:S(2)}) collective-permute-start(bf16[208,1280]{1,0:T(8,128)(2,1)S(1)} %get-tuple-element.18), channel_id=1, source_target_pairs={{2,6},{6,10},{10,14},{3,7},{7,11},{11,15},{18,22},{22,26},{26,30},... | collective-permute-start | bytes 1597448 | tf_op jit(solution)/shard_map/ppermute | solution.py:28
  3.0 37.5 %collective-permute-start = (bf16[208,1280]{1,0:T(8,128)(2,1)S(1)}, bf16[208,1280]{1,0:T(8,128)(2,1)S(1)}, u32[]{:S(2)}, u32[]{:S(2)}) collective-permute-start(bf16[208,1280]{1,0:T(8,128)(2,1)S(1)} %get-tuple-element.18), channel_id=1, source_target_pairs={{0,2},{2,0},{4,6},{6,4},{8,10},{10,8},{12,14},{14,12},{1,3},{3,1},... | collective-permute-start | bytes 1597448 | tf_op jit(solution)/shard_map/ppermute | solution.py:28
  8.9 1.2 %collective-permute-start.3 = (f32[8,208]{1,0:T(8,128)S(1)}, f32[8,208]{1,0:T(8,128)S(1)}, u32[]{:S(2)}, u32[]{:S(2)}) collective-permute-start(f32[8,208]{1,0:T(8,128)S(1)} %get-tuple-element.20.own_ref), channel_id=1, source_target_pairs={{0,1},{1,0},{2,3},{3,2},{4,5},{5,4},{6,7},{7,6},{8,9},{9,8},{10,11... | collective-permute-start | bytes 19976 | tf_op jit(solution)/shard_map/ppermute | solution.py:33
  8.9 25.1 %collective-permute-start.10 = (bf16[208,1280]{1,0:T(8,128)(2,1)S(1)}, bf16[208,1280]{1,0:T(8,128)(2,1)S(1)}, u32[]{:S(2)}, u32[]{:S(2)}) collective-permute-start(bf16[208,1280]{1,0:T(8,128)(2,1)S(1)} %get-tuple-element.29), channel_id=1, source_target_pairs={{0,2},{2,0},{4,6},{6,4},{8,10},{10,8},{12,14},{14,12},{1,3},{3,1},... | collective-permute-start | bytes 1597448 | tf_op jit(solution)/shard_map/ppermute | solution.py:28
  9.0 8.0 %copy-start.4 = (bf16[1,20,128,128]{3,2,1,0:T(8,128)(2,1)S(1)}, bf16[1,20,128,128]{3,2,1,0:T(8,128)(2,1)}, u32[]{:S(2)}) copy-start(bf16[1,20,128,128]{3,2,1,0:T(8,128)(2,1)} %k_hbm.1) | copy-start | bytes 1966084
  12.7 24.9 %copy-start.5 = (bf16[1,20,128,128]{3,2,1,0:T(8,128)(2,1)S(1)}, bf16[1,20,128,128]{3,2,1,0:T(8,128)(2,1)}, u32[]{:S(2)}) copy-start(bf16[1,20,128,128]{3,2,1,0:T(8,128)(2,1)} %q_hbm.1) | copy-start | bytes 1966084
  12.7 1.2 %collective-permute-start.4 = (f32[8,208]{1,0:T(8,128)S(1)}, f32[8,208]{1,0:T(8,128)S(1)}, u32[]{:S(2)}, u32[]{:S(2)}) collective-permute-start(f32[8,208]{1,0:T(8,128)S(1)} %token_squares.1), channel_id=1, source_target_pairs={{0,1},{1,0},{2,3},{3,2},{4,5},{5,4},{6,7},{7,6},{8,9},{9,8},{10,11... | collective-permute-start | bytes 19976 | tf_op jit(solution)/shard_map/ppermute | solution.py:33
  14.0 6.5 %collective-permute-start.7 = (f32[8,208]{1,0:T(8,128)S(1)}, f32[8,208]{1,0:T(8,128)S(1)}, u32[]{:S(2)}, u32[]{:S(2)}) collective-permute-start(f32[8,208]{1,0:T(8,128)S(1)} %multiply_select_fusion.own_ref), channel_id=1, source_target_pairs={{0,14},{2,4},{4,2},{6,8},{8,6},{10,12},{12,10},{14,0},{1,15},{3,5}... | collective-permute-start | bytes 19976 | tf_op jit(solution)/shard_map/ppermute | solution.py:28
  16.5 15.9 %collective-permute-start.6 = (f32[8,208]{1,0:T(8,128)S(1)}, f32[8,208]{1,0:T(8,128)S(1)}, u32[]{:S(2)}, u32[]{:S(2)}) collective-permute-start(f32[8,208]{1,0:T(8,128)S(1)} %multiply_select_fusion.own_ref), channel_id=1, source_target_pairs={{0,2},{2,0},{4,6},{6,4},{8,10},{10,8},{12,14},{14,12},{1,3},{3,1},... | collective-permute-start | bytes 19976 | tf_op jit(solution)/shard_map/ppermute | solution.py:28
  20.4 22.9 %collective-permute-start.11 = (bf16[208,1280]{1,0:T(8,128)(2,1)S(1)}, bf16[208,1280]{1,0:T(8,128)(2,1)S(1)}, u32[]{:S(2)}, u32[]{:S(2)}) collective-permute-start(bf16[208,1280]{1,0:T(8,128)(2,1)S(1)} %get-tuple-element.29), channel_id=1, source_target_pairs={{0,4},{2,6},{4,8},{6,10},{8,12},{10,14},{1,5},{3,7},{5,9},{7,11},{... | collective-permute-start | bytes 1597448 | tf_op jit(solution)/shard_map/ppermute | solution.py:28
  32.4 5.7 %collective-permute-start.5 = (f32[8,208]{1,0:T(8,128)S(1)}, f32[8,208]{1,0:T(8,128)S(1)}, u32[]{:S(2)}, u32[]{:S(2)}) collective-permute-start(f32[8,208]{1,0:T(8,128)S(1)} %multiply_select_fusion.own_ref), channel_id=1, source_target_pairs={{0,4},{2,6},{4,8},{6,10},{8,12},{10,14},{12,0},{14,2},{1,5},{3,7},... | collective-permute-start | bytes 19976 | tf_op jit(solution)/shard_map/ppermute | solution.py:28
  34.0 15.9 %collective-permute-start.12 = (bf16[208,1280]{1,0:T(8,128)(2,1)S(1)}, bf16[208,1280]{1,0:T(8,128)(2,1)S(1)}, u32[]{:S(2)}, u32[]{:S(2)}) collective-permute-start(bf16[208,1280]{1,0:T(8,128)(2,1)S(1)} %collective-permute-done.10.near_ref), channel_id=1, source_target_pairs={{0,4},{4,8},{6,2},{8,12},{10,6},{14,10},{1,5},{5,9},{7,3},{9,13},{... | collective-permute-start | bytes 1597448 | tf_op jit(solution)/shard_map/ppermute | solution.py:28
  38.1 3.9 %copy-start.3 = (s32[8]{0:T(128)S(1)}, s32[8]{0:T(128)}, u32[]{:S(2)}) copy-start(s32[8]{0:T(128)} %pos_ref.1) | copy-start | bytes 100
  38.1 11.8 %copy-start.1 = (f32[1,3,2560]{2,0,1:T(1,128)S(1)}, f32[1,3,2560]{2,0,1:T(1,128)}, u32[]{:S(2)}) copy-start(f32[1,3,2560]{2,0,1:T(1,128)} %param.13) | copy-start | bytes 92164
  38.1 11.8 %copy-start.2 = (f32[1,3,2560]{2,0,1:T(1,128)S(1)}, f32[1,3,2560]{2,0,1:T(1,128)}, u32[]{:S(2)}) copy-start(f32[1,3,2560]{2,0,1:T(1,128)} %param.14) | copy-start | bytes 92164
  38.1 20.9 %collective-permute-start.8 = (bf16[208,1280]{1,0:T(8,128)(2,1)S(1)}, bf16[208,1280]{1,0:T(8,128)(2,1)S(1)}, u32[]{:S(2)}, u32[]{:S(2)}) collective-permute-start(bf16[208,1280]{1,0:T(8,128)(2,1)S(1)} %get-tuple-element.18), channel_id=1, source_target_pairs={{0,4},{4,8},{8,12},{1,5},{5,9},{9,13},{16,20},{20,24},{24,28},{17,... | collective-permute-start | bytes 1597448 | tf_op jit(solution)/shard_map/ppermute | solution.py:28
  40.1 19.0 %collective-permute-start.9 = (bf16[208,1280]{1,0:T(8,128)(2,1)S(1)}, bf16[208,1280]{1,0:T(8,128)(2,1)S(1)}, u32[]{:S(2)}, u32[]{:S(2)}) collective-permute-start(bf16[208,1280]{1,0:T(8,128)(2,1)S(1)} %collective-permute-done.1.ahead_ref), channel_id=1, source_target_pairs={{0,2},{2,0},{4,6},{6,4},{8,10},{10,8},{12,14},{14,12},{1,3},{3,1},... | collective-permute-start | bytes 1597448 | tf_op jit(solution)/shard_map/ppermute | solution.py:28
  40.5 18.6 %collective-permute-start.2 = (bf16[208,1280]{1,0:T(8,128)(2,1)S(1)}, bf16[208,1280]{1,0:T(8,128)(2,1)S(1)}, u32[]{:S(2)}, u32[]{:S(2)}) collective-permute-start(bf16[208,1280]{1,0:T(8,128)(2,1)S(1)} %collective-permute-done.near_ref), channel_id=1, source_target_pairs={{6,2},{10,6},{14,10},{7,3},{11,7},{15,11},{22,18},{26,22},{30,26},... | collective-permute-start | bytes 1597448 | tf_op jit(solution)/shard_map/ppermute | solution.py:28
